TPU v7x, 256 devices: a whole 4x4x8 slice. The times are simulated.
256 devices in a mesh: dp: 8 (over z_hi, x), space: 32 (over z_lo, y, core).
Axes of the slice: x: 4, y: 4, z: 8 (z_hi: 2, z_lo: 4; z = z_hi * 4 + z_lo), core: 2. Of those that a mesh axis runs over, the one named last changes fastest.
Arguments:
- crop: bfloat16 [8, 4, 128, 64, 64], P('dp', None, 'space'), may hold values from -6 to 6
- filter_one: bfloat16 [3, 3, 3, 4, 32], replicated, may hold values from -0.625 to 0.625
- filter_two: bfloat16 [3, 3, 3, 32, 64], replicated, may hold values from -0.21875 to 0.21875
- cotangent: bfloat16 [8, 64, 32, 16, 16], P('dp', None, 'space'), may hold values from -1 to 1
Outputs:
- features: bfloat16 [8, 64, 32, 16, 16], P('dp', None, 'space')
- grad_one: float32 [3, 3, 3, 4, 32], replicated
- grad_two: float32 [3, 3, 3, 32, 64], replicated
All inputs are finite; a program needn't handle non-finite values.
Results may differ from a plain program's by a relative error of at most 0.0045.
The roundings to bfloat16 on the way count: a program that leaves them out, or rounds other values in their place, can miss the bound.
Values may be sent and summed in bfloat16 or wider, within the bound.
A program may use at most 128 MiB of HBM per device.

v0:
```python
import jax
import jax.numpy as jnp
from jax import lax
from jax.sharding import PartitionSpec as P


def with_halo(shard, sides, width):
    for axis, dim in sides:
        count, length = (lax.axis_size(axis), shard.shape[dim])
        up = [(i, (i + 1) % count) for i in range(count - 1)]
        down = [(j, i) for i, j in up]
        last = lax.slice_in_dim(shard, length - width, length, axis=dim)
        leading = lax.slice_in_dim(shard, 0, width, axis=dim)
        before = lax.ppermute(last, axis, up)
        after = lax.ppermute(leading, axis, down)
        shard = jnp.concatenate([before, shard, after], axis=dim)
    return shard


def leaky(value):
    return jnp.where(value > 0, value, 0.3 * value)


def slope(value):
    return jnp.where(value > 0, 1.0, 0.3)


def pooled(value):
    shape = value.shape
    blocks = value.reshape(shape[0], shape[1], shape[2] // 2, 2, shape[3] // 2, 2, shape[4] // 2, 2)
    return blocks.mean(axis=(3, 5, 7))


def widened(value):
    shape = value.shape
    spread = jnp.broadcast_to(
        value[:, :, :, None, :, None, :, None],
        (shape[0], shape[1], shape[2], 2, shape[3], 2, shape[4], 2),
    )
    return spread.reshape(shape[0], shape[1], 2 * shape[2], 2 * shape[3], 2 * shape[4])


def convolve(source, kernel):
    return lax.conv_general_dilated(
        source,
        kernel,
        (1, 1, 1),
        ((0, 0), (1, 1), (1, 1)),
        dimension_numbers=("NCDHW", "DHWIO", "NCDHW"),
        preferred_element_type=jnp.float32,
    )


def flipped(kernel):
    return jnp.transpose(kernel[::-1, ::-1, ::-1], (0, 1, 2, 4, 3))


def filter_grad(source, gradient):
    planes, extent_y, extent_z = (gradient.shape[2], gradient.shape[3], gradient.shape[4])
    padded = jnp.pad(source, ((0, 0), (0, 0), (0, 0), (1, 1), (1, 1)))
    partials = []
    for offset in range(27):
        shift_a, shift_b, shift_c = (offset // 9, offset // 3 % 3, offset % 3)
        window = padded[
            :,
            :,
            shift_a : shift_a + planes,
            shift_b : shift_b + extent_y,
            shift_c : shift_c + extent_z,
        ]
        partials.append(
            jnp.einsum("bcxyz,bdxyz->cd", window, gradient, preferred_element_type=jnp.float32)
        )
    return jnp.stack(partials).reshape(3, 3, 3, source.shape[1], gradient.shape[1])


def local(crop, filter_one, filter_two, cotangent):
    crop_wide = with_halo(crop, (("space", 2),), 1)
    z_one = convolve(crop_wide, filter_one)
    maps_one = pooled(leaky(z_one)).astype(jnp.bfloat16)
    maps_wide = with_halo(maps_one, (("space", 2),), 1)
    z_two = convolve(maps_wide, filter_two)
    grad_pre_two = (slope(z_two) * widened(cotangent.astype(jnp.float32)) * 0.125).astype(
        jnp.bfloat16
    )
    grad_outer = with_halo(grad_pre_two, (("space", 2),), 1)
    features = pooled(leaky(z_two)).astype(jnp.bfloat16)
    local_two = filter_grad(maps_wide, grad_pre_two)
    back_one = convolve(grad_outer, flipped(filter_two))
    grad_pre_one = (slope(z_one) * widened(back_one) * 0.125).astype(jnp.bfloat16)
    local_one = filter_grad(crop_wide, grad_pre_one)
    grad_one, grad_two = lax.psum((local_one, local_two), ("dp", "space"))
    return (features, grad_one, grad_two)


def solution(mesh):
    placed = (P("dp", None, "space", None, None), P(), P(), P("dp", None, "space", None, None))
    return jax.shard_map(
        local,
        mesh=mesh,
        in_specs=placed,
        out_specs=(P("dp", None, "space", None, None), P(), P()),
        check_vma=False,
    )
```

profile of v0, /device:TPU:1, one launch (start us, length us, event | category | flops | bytes accessed | tf_op | source)
XLA Modules:
  0.0 399.3 jit_solution(16076839817375526808)
XLA Ops:
  7.2 1.2 copy.322
  8.5 4.6 %collective-permute-start = (bf16[1,4,1,64,64]{4,1,3,2,0:T(4,128)(2,1)S(1)}, bf16[1,4,1,64,64]{4,1,3,2,0:T(4,128)(2,1)S(1)}, u32[]{:S(2)}, u32[]{:S(2)}) collective-permute-start(bf16[1,4,1,64,64]{4,1,3,2,0:T(4,128)(2,1)S(1)} %get-tuple-element.20), channel_id=1, source_target_pairs={{0,1},{1,2},{2,3},{3,4},{4,5},{5,6},{6,7},{7,8},{8,9},{9,10},{10,1... | collective-permute-start | bytes 98312 | tf_op jit(solution)/shard_map/ppermute | solution.py:14
  13.1 1.9 collective-permute-start.1
  15.7 1.2 constant_dynamic-update-slice_fusion.1
  16.9 1.8 collective-permute-done.1
  19.8 3.7 copy.327
  23.6 1.7 slice.254
  25.2 24.3 %compare_select_fusion = (f32[4,64,8,9,32]{4,2,3,1,0:T(8,128)}, f32[4,64,8,9,32]{4,2,3,1,0:T(8,128)}) fusion(pred[8,9]{0,1:T(8,128)(4,1)S(1)} %copy-done.15, bf16[3,3,3,4,32]{4,3,2,1,0:T(4,128)(2,1)S(1)} %copy-done.14, bf16[4,6,64,1,7,2]{4,0,5,2,1,3:T(4,128)(2,1)S(1)} %slice.254, bf16[4,6,64,1,8,9]{4,0,5,2,1,3:T(4,128)(2,1)} %copy.327), kind=kOutput, calls=%fused_computation.1 | convolution fusion | flops 129835008 | bytes 4989768 | tf_op jit(solution)/shard_map/conv_general_dilated | solution.py:44
  49.5 8.7 %copy.328 = f32[4,64,8,9,32]{1,4,3,2,0:T(8,128)} copy(f32[4,64,8,9,32]{4,2,3,1,0:T(8,128)} %get-tuple-element.10) | data formatting | bytes 4718592 | tf_op jit(solution)/shard_map/jit(_where)/select_n | solution.py:21
  58.2 4.6 %slice_bitcast_fusion.1 = f32[1,32,4,64,64]{3,1,4,2,0:T(8,128)} fusion(f32[4,64,1,72,32]{1,4,3,0,2:T(8,128)} %bitcast.701), kind=kLoop, calls=%fused_computation.14 | loop fusion | bytes 4194304 | tf_op jit(solution)/shard_map/jit(_where)/select_n | solution.py:21
  62.8 9.3 %copy.329 = f32[1,32,4,64,64]{1,4,3,2,0:T(8,128)} copy(f32[1,32,4,64,64]{3,1,4,2,0:T(8,128)} %slice_bitcast_fusion.1) | data formatting | bytes 4194304 | tf_op jit(solution)/shard_map/jit(_where)/select_n | solution.py:21
  72.1 9.1 %reduce_sum.21 = f32[32,2,32,32]{0,3,2,1:T(8,128)S(1)} reduce(f32[32,2,2,32,2,32,2]{0,6,5,4,3,2,1:T(2,128)} %bitcast.698, f32[]{:T(128)} %constant.5.clone.1), dimensions={2,4,6}, to_apply=%region_0.1 | reduce | flops 458752 | bytes 2359300 | tf_op jit(solution)/shard_map/reduce_sum | solution.py:31
  81.7 0.7 fusion.295
  82.5 1.9 collective-permute-start.2
  84.4 2.4 collective-permute-start.3
  87.5 0.9 copy.357
  88.4 8.7 %copy.335 = f32[4,64,8,9,32]{1,4,3,2,0:T(8,128)} copy(f32[4,64,8,9,32]{4,2,3,1,0:T(8,128)} %get-tuple-element.9) | data formatting | bytes 4718592 | tf_op jit(solution)/shard_map/jit(_where)/select_n | solution.py:25
  97.8 2.3 pad_maximum_fusion
  100.1 3.8 copy.455
  103.9 2.6 pad.12.clone
  106.5 3.0 copy.333
  109.5 1.2 slice.258
  110.7 4.6 %compare_select_fusion.1 = (f32[2,32,8,5,64]{4,2,3,1,0:T(8,128)S(1)}, f32[2,32,8,5,64]{4,2,3,1,0:T(8,128)}) fusion(bf16[3,3,3,32,64]{4,3,2,1,0:T(8,128)(2,1)S(1)} %copy-done, bf16[32,4,32,1,7,2]{0,4,5,2,1,3:T(8,128)(2,1)S(1)} %slice.258, bf16[32,4,32,1,8,5]{0,4,5,2,1,3:T(8,128)(2,1)} %copy.333, pred[8,5]{0,1:T(8,128)(4,1)S(1)} %copy-done.16), kind=kOutput, calls=%fused_computation.34 | convolution fusion | flops 279412736 | bytes 1863720 | tf_op jit(solution)/shard_map/conv_general_dilated | solution.py:44
  116.7 1.0 fusion.91
  131.9 1.5 fusion.39
  136.0 0.8 copy-done.5
  136.9 3.1 collective-permute-start.4
  140.0 2.1 collective-permute-start.5
  142.1 1.6 copy.334
  144.9 2.8 collective-permute-done.5
  148.9 5.1 %fusion.32 = f32[2,32,8,5,32]{4,2,3,1,0:T(8,128)S(1)} fusion(bf16[3,3,3,32,64]{4,3,2,1,0:T(8,128)(2,1)S(1)} %copy-done, bf16[64,4,32,1,7,2]{0,4,5,2,1,3:T(8,128)(2,1)S(1)} %slice.264, bf16[64,4,32,1,8,5]{0,4,5,2,1,3:T(8,128)(2,1)S(1)} %copy.339, pred[8,5]{0,1:T(8,128)(4,1)S(1)} %copy-done.16), kind=kOutput, calls=%fused_computation.36 | convolution fusion | flops 280051712 | bytes 1323048 | tf_op jit(solution)/shard_map/conv_general_dilated | solution.py:44
  155.0 7.6 %broadcast_in_dim.44 = f32[32,2,2,32,2,32,2]{0,6,5,4,3,2,1:T(2,128)} broadcast(f32[32,2,32,32]{0,3,2,1:T(8,128)S(1)} %copy.341), dimensions={0,1,3,5} | broadcast | bytes 2359296 | tf_op jit(solution)/shard_map/broadcast_in_dim | solution.py:36
  162.6 7.8 %copy.342 = f32[1,32,4,64,64]{3,1,4,2,0:T(8,128)} copy(f32[1,32,4,64,64]{1,4,3,2,0:T(8,128)} %bitcast.699) | data formatting | bytes 4194304 | tf_op jit(solution)/shard_map/broadcast_in_dim | solution.py:36
  170.4 5.8 %fusion.14 = bf16[32,4,64,64]{2,0,3,1:T(8,128)(2,1)} fusion(f32[1,32,4,64,64]{3,1,4,2,0:T(8,128)} %copy.342, f32[4,64,1,72,32]{1,4,3,0,2:T(8,128)} %bitcast.700), kind=kLoop, calls=%fused_computation.20 | loop fusion | flops 1572864 | bytes 5242880 | tf_op jit(solution)/shard_map/reshape.3
  176.3 5.7 %copy.343 = bf16[32,4,64,64]{3,0,2,1:T(8,128)(2,1)S(1)} copy(bf16[32,4,64,64]{2,0,3,1:T(8,128)(2,1)} %fusion.14) | data formatting | bytes 2097152 | tf_op jit(solution)/shard_map/reshape.3
  184.0 0.7 fusion.85
  185.4 0.7 fusion.83
  186.1 0.7 fusion.82
  188.3 0.7 fusion.79
  190.4 0.7 fusion.76
  191.9 0.7 fusion.74
  192.6 0.7 fusion.73
  196.9 0.7 fusion.67
  198.3 0.7 fusion.65
  199.0 0.7 fusion.64
  201.1 85.7 %psum.14 = f32[3,3,3,4,32]{4,3,2,1,0:T(4,128)} all-reduce(f32[3,3,3,4,32]{4,3,2,1,0:T(4,128)S(1)} %bitcast.714), channel_id=1, replica_groups=mesh['dp'=8,'space'=32] {'dp','space'}, use_global_device_ids=true, to_apply=%region_3.4 | all-reduce | flops 3456 | bytes 27648 | tf_op jit(solution)/shard_map/psum | solution.py:92
  286.8 103.6 %all-reduce.4.cloned.1.call-done = f32[3,3,3,32,64]{4,3,2,1,0:T(8,128)} async-done(((f32[3,3,3,32,64]{4,3,2,1,0:T(8,128)}), f32[3,3,3,32,64]{4,3,2,1,0:T(8,128)}) %all-reduce.4.cloned.1.call-update) | async-done | bytes 221200 | tf_op jit(solution)/shard_map/psum | solution.py:92
  390.4 1.8 copy.566
  (106 shorter events, 36.9 us)
Async XLA Ops:
  7.2 103.6 %copy-start = (bf16[3,3,3,32,64]{4,3,2,1,0:T(8,128)(2,1)S(1)}, bf16[3,3,3,32,64]{4,3,2,1,0:T(8,128)(2,1)}, u32[]{:S(2)}) copy-start(bf16[3,3,3,32,64]{4,3,2,1,0:T(8,128)(2,1)} %param.6) | copy-start | bytes 331780
  7.2 383.2 %all-reduce.4.cloned.1.call-start = ((), (), s32[]{:S(2)}) async-start(), calls=%async_computation | async-start | bytes 884736 | tf_op jit(solution)/shard_map/psum | solution.py:92
  8.5 6.5 %collective-permute-start = (bf16[1,4,1,64,64]{4,1,3,2,0:T(4,128)(2,1)S(1)}, bf16[1,4,1,64,64]{4,1,3,2,0:T(4,128)(2,1)S(1)}, u32[]{:S(2)}, u32[]{:S(2)}) collective-permute-start(bf16[1,4,1,64,64]{4,1,3,2,0:T(4,128)(2,1)S(1)} %get-tuple-element.20), channel_id=1, source_target_pairs={{0,1},{1,2},{2,3},{3,4},{4,5},{5,6},{6,7},{7,8},{8,9},{9,10},{10,1... | collective-permute-start | bytes 98312 | tf_op jit(solution)/shard_map/ppermute | solution.py:14
  13.1 5.6 %collective-permute-start.1 = (bf16[1,4,1,64,64]{4,1,3,2,0:T(4,128)(2,1)S(1)}, bf16[1,4,1,64,64]{4,1,3,2,0:T(4,128)(2,1)S(1)}, u32[]{:S(2)}, u32[]{:S(2)}) collective-permute-start(bf16[1,4,1,64,64]{4,1,3,2,0:T(4,128)(2,1)S(1)} %get-tuple-element.19), channel_id=1, source_target_pairs={{1,0},{2,1},{3,2},{4,3},{5,4},{6,5},{7,6},{8,7},{9,8},{10,9},{11,1... | collective-permute-start | bytes 98312 | tf_op jit(solution)/shard_map/ppermute | solution.py:15
  15.0 0.6 copy-start.10
  18.7 0.6 copy-start.8
  19.8 5.4 %copy-start.14 = (bf16[3,3,3,4,32]{4,3,2,1,0:T(4,128)(2,1)S(1)}, bf16[3,3,3,4,32]{4,3,2,1,0:T(4,128)(2,1)}, u32[]{:S(2)}) copy-start(bf16[3,3,3,4,32]{4,3,2,1,0:T(4,128)(2,1)} %param.5) | copy-start | bytes 20740
  19.8 5.4 %copy-start.15 = (pred[8,9]{0,1:T(8,128)(4,1)S(1)}, pred[8,9]{0,1:T(8,128)(4,1)}, u32[]{:S(2)}) copy-start(pred[8,9]{0,1:T(8,128)(4,1)} %constant.39) | copy-start | bytes 220
  81.6 5.2 %copy-start.13 = (bf16[1,64,1,16,16]{1,4,3,2,0:T(8,128)(2,1)S(1)}, bf16[1,64,1,16,16]{1,4,3,2,0:T(8,128)(2,1)}, u32[]{:S(2)}) copy-start(bf16[1,64,1,16,16]{1,4,3,2,0:T(8,128)(2,1)} %param.7) | copy-start | bytes 98308
  81.6 5.9 %copy-start.3 = (bf16[1,4,4,64,64]{4,3,2,1,0:T(8,128)(2,1)S(1)}, bf16[1,4,4,64,64]{4,3,2,1,0:T(8,128)(2,1)}, u32[]{:S(2)}) copy-start(bf16[1,4,4,64,64]{4,3,2,1,0:T(8,128)(2,1)} %param.4) | copy-start | bytes 393220
  82.5 14.6 %collective-permute-start.2 = (bf16[1,32,1,32,32]{4,1,3,2,0:T(8,128)(2,1)}, bf16[1,32,1,32,32]{4,1,3,2,0:T(8,128)(2,1)S(1)}, u32[]{:S(2)}, u32[]{:S(2)}) collective-permute-start(bf16[1,32,1,32,32]{4,1,3,2,0:T(8,128)(2,1)} %get-tuple-element.17), channel_id=1, source_target_pairs={{0,1},{1,2},{2,3},{3,4},{4,5},{5,6},{6,7},{7,8},{8,9},{9,10},{10,1... | collective-permute-start | bytes 196616 | tf_op jit(solution)/shard_map/ppermute | solution.py:14
  84.4 13.4 %collective-permute-start.3 = (bf16[1,32,1,32,32]{4,1,3,2,0:T(8,128)(2,1)S(1)}, bf16[1,32,1,32,32]{4,1,3,2,0:T(8,128)(2,1)}, u32[]{:S(2)}, u32[]{:S(2)}) collective-permute-start(bf16[1,32,1,32,32]{4,1,3,2,0:T(8,128)(2,1)S(1)} %get-tuple-element.18), channel_id=1, source_target_pairs={{1,0},{2,1},{3,2},{4,3},{5,4},{6,5},{7,6},{8,7},{9,8},{10,9},{11,1... | collective-permute-start | bytes 196616 | tf_op jit(solution)/shard_map/ppermute | solution.py:15
  97.1 0.7 copy-start.6
  106.5 4.2 %copy-start.16 = (pred[8,5]{0,1:T(8,128)(4,1)S(1)}, pred[8,5]{0,1:T(8,128)(4,1)}, u32[]{:S(2)}) copy-start(pred[8,5]{0,1:T(8,128)(4,1)} %constant.38) | copy-start | bytes 124
  115.4 0.9 copy-start.4
  118.3 1.9 copy-start.7
  134.8 2.0 copy-start.2
  136.0 0.8 copy-start.5
  136.9 8.1 %collective-permute-start.4 = (bf16[1,64,1,32,32]{1,3,4,2,0:T(8,128)(2,1)S(1)}, bf16[1,64,1,32,32]{1,3,4,2,0:T(8,128)(2,1)S(1)}, u32[]{:S(2)}, u32[]{:S(2)}) collective-permute-start(bf16[1,64,1,32,32]{1,3,4,2,0:T(8,128)(2,1)S(1)} %get-tuple-element.15), channel_id=1, source_target_pairs={{0,1},{1,2},{2,3},{3,4},{4,5},{5,6},{6,7},{7,8},{8,9},{9,10},{10,1... | collective-permute-start | bytes 393224 | tf_op jit(solution)/shard_map/ppermute | solution.py:14
  140.0 7.7 %collective-permute-start.5 = (bf16[1,64,1,32,32]{1,3,4,2,0:T(8,128)(2,1)S(1)}, bf16[1,64,1,32,32]{1,3,4,2,0:T(8,128)(2,1)S(1)}, u32[]{:S(2)}, u32[]{:S(2)}) collective-permute-start(bf16[1,64,1,32,32]{1,3,4,2,0:T(8,128)(2,1)S(1)} %get-tuple-element.16), channel_id=1, source_target_pairs={{1,0},{2,1},{3,2},{4,3},{5,4},{6,5},{7,6},{8,7},{9,8},{10,9},{11,1... | collective-permute-start | bytes 393224 | tf_op jit(solution)/shard_map/ppermute | solution.py:15
  183.3 1.5 copy-start.11
  189.6 1.6 copy-start.1
  189.6 1.6 copy-start.12
  196.1 1.5 copy-start.9
Sparse Core Ops, SparseCore 0:
  136.9 253.4 all-reduce.3
where the time goes:
time: 407 us; the launch traced here: 399 us
  waiting for transfers between devices  108 us (27%)
  blocking collectives  85.7 us (21%)
  local copies, waits for them, and re-layouts  83.9 us (21%)
  matrix products  71.1 us (17%)
  other arithmetic  19.3 us (5%)
  starting transfers between devices  16.1 us (4%)
  between operations  14.9 us (4%)
    psum x1, waiting for transfers between devices, local(): grad_one, grad_two = lax.psum((local_one, local_two), ('dp', 'space'))  104 us
    psum x1, blocking collectives, local(): grad_one, grad_two = lax.psum((local_one, local_two), ('dp', 'space'))  85.7 us
    dot_general x54, matrix products, filter_grad(): jnp.einsum('bcxyz,bdxyz->cd', window, gradient, preferred_element_type=jn...  37.1 us
    conv_general_dilated x3, matrix products, convolve(): lax.conv_general_dilated(source, kernel, (1, 1, 1), ((0, 0), (1, 1), (1,...  34 us
    select_n x4, local copies, waits for them, and re-layouts, leaky(): return jnp.where(value > 0, value, 0.3 * value)  24.2 us
    broadcast_in_dim x6, local copies, waits for them, and re-layouts, widened(): jnp.broadcast_to(value[:, :, :, None, :, None, :, None], (shape[0], shape...  17.1 us
    unnamed x41, local copies, waits for them, and re-layouts  12.5 us
    conv_general_dilated x7, local copies, waits for them, and re-layouts, convolve(): lax.conv_general_dilated(source, kernel, (1, 1, 1), ((0, 0), (1, 1), (1,...  10.5 us
  transfers between devices with their start and end apart: 7, of which 3 were waited for; matrix products, arithmetic and copies ran while one was open for 17% of the time, Pallas kernels for 0%

commit v1 on v0

v1 whole, which is shorter than its diff:
```python
import functools

import jax
import jax.numpy as jnp
import numpy as np
from jax import lax
from jax.experimental import pallas as pl
from jax.experimental.pallas import tpu as pltpu
from jax.sharding import PartitionSpec as P

F32, BF16 = jnp.float32, jnp.bfloat16
LANES = 1024


def leaky(value):
    return jnp.where(value > 0, value, 0.3 * value)


def dot_nn(a, b):
    return lax.dot_general(a, b, (((1,), (0,)), ((), ())), preferred_element_type=F32)


def dot_nt(a, b):
    return lax.dot_general(a, b, (((1,), (1,)), ((), ())), preferred_element_type=F32)


def split2(value):
    high = value.astype(BF16)
    return high, (value - high.astype(F32)).astype(BF16)


def tap_selection():
    table = np.zeros((128, 8, 256), np.float32)
    for d in range(8):
        dp, dq, dr = d // 4, d // 2 % 2, d % 2
        for pi in range(4):
            for sq in range(2):
                for sr in range(2):
                    for qe in range(2):
                        for re in range(2):
                            qi = (1 + qe) if sq == 0 else (0 if qe else 3)
                            ri = (1 + re) if sr == 0 else (0 if re else 3)
                            a, b, c = pi - dp, qi - dq, ri - dr
                            if min(a, b, c) < 0 or max(a, b, c) > 2:
                                continue
                            for i in range(4):
                                k = pi * 64 + (sq * 2 + sr) * 16 + (qe * 2 + re) * 4 + i
                                table[((a * 3 + b) * 3 + c) * 4 + i, d, k] = 1
    return table.reshape(128, 2048)


def lane_masks(rows):
    lane = lax.broadcasted_iota(jnp.int32, (rows, LANES), 1)
    return lane % 32, lane // 32


def ones(mask):
    return jnp.where(mask, 1.0, 0.0).astype(BF16)


def rolled(value, amount):
    return pltpu.roll(value, amount % LANES, 1)


def compute(first, s, crop_ref, w1_ref, w2_ref, w3_ref, sel_ref, cot_ref, feat_ref, g2_out, g1_out,
            px, maps, z1s, g2s, g1s):
    r, q = lane_masks(16)
    row = lax.broadcasted_iota(jnp.int32, (16, LANES), 0)
    q_odd, r_odd = row // 8 == 1, row // 4 % 2 == 1
    r_up, r_down = ones(r_odd & (r != 0)), ones(~r_odd & (r != 31))
    q_up, q_down = ones(q_odd & (q != 0)), ones(~q_odd & (q != 31))
    for plane in range(14):
        x = crop_ref[plane]
        xr = rolled(x, 1) * r_up + rolled(x, -1) * r_down
        xq = rolled(x, 32) * q_up + rolled(x, -32) * q_down
        xqr = rolled(xr, 32) * q_up + rolled(xr, -32) * q_down
        for k, piece in enumerate((x, xr, xq, xqr)):
            px[plane * 64 + k * 16 : plane * 64 + k * 16 + 16, :] = piece
    w1 = w1_ref[...]
    r, q = lane_masks(32)
    keep, keep_ones = {}, {}
    for db in (-1, 0, 1):
        for dc in (-1, 0, 1):
            ok = jnp.ones((32, LANES), jnp.bool_)
            if db:
                ok = ok & ((q != 0) if db < 0 else (q != 31))
            if dc:
                ok = ok & ((r != 0) if dc < 0 else (r != 31))
            keep[db, dc] = ok
            keep_ones[db, dc] = ones(ok)
    left_ok = jnp.where(s > 0, 1.0, 0.0)
    right_ok = jnp.where(s < 31, 1.0, 0.0)
    for plane in range(6):
        z = dot_nn(w1, px[plane * 128 : plane * 128 + 256, :])
        if plane in (2, 3):
            z1s[(plane - 2) * 256 : (plane - 1) * 256, :] = z.astype(BF16)
        z = leaky(z)
        total = z[0:32]
        for d in range(1, 8):
            total = total + z[d * 32 : d * 32 + 32]
        scale = 0.125 * (left_ok if plane < 2 else right_ok if plane > 3 else 1.0)
        a1 = (total * scale).astype(BF16)
        for b in range(3):
            for c in range(3):
                v = a1
                if (b, c) != (1, 1):
                    v = rolled(v, -(32 * (b - 1) + (c - 1)))
                    v = v * keep_ones[b - 1, c - 1]
                at = plane * 288 + (b * 3 + c) * 32
                maps[at : at + 32, :] = v
    k_id = lax.broadcasted_iota(jnp.int32, (128, 512), 0)
    n_id = lax.broadcasted_iota(jnp.int32, (128, 512), 1)
    spread = ((n_id // 64 == k_id // 16) & (n_id % 32 // 2 == k_id % 16)).astype(F32).astype(BF16)
    pk = lax.broadcasted_iota(jnp.int32, (256, 64), 0)
    pn = lax.broadcasted_iota(jnp.int32, (256, 64), 1)
    gather = ((pk // 64 == pn // 16) & (pk % 32 // 2 == pn % 16)).astype(F32).astype(BF16)
    w2 = w2_ref[...]
    pair = None
    for plane in range(4):
        z = dot_nn(w2, maps[plane * 288 : plane * 288 + 864, :])
        cot = cot_ref[(0, 1, 1, 2)[plane]]
        wide = jnp.concatenate([dot_nn(cot[:, 0:128], spread), dot_nn(cot[:, 128:256], spread)], axis=1) * 0.125
        g2s[plane * 64 : plane * 64 + 64, :] = jnp.where(z > 0, wide, 0.3 * wide).astype(BF16)
        if plane == 1:
            pair = leaky(z)
        elif plane == 2:
            pair = pair + leaky(z)
            high, low = split2(pair)
            for j in range(4):
                lanes = slice(256 * j, 256 * j + 256)
                feat_ref[:, 64 * j : 64 * j + 64] = (
                    (dot_nn(high[:, lanes], gather) + dot_nn(low[:, lanes], gather)) * 0.125
                ).astype(BF16)
    grad = dot_nt(maps[288 : 288 + 864, :], g2s[64:128, :])
    grad = grad + dot_nt(maps[576 : 576 + 864, :], g2s[128:192, :])
    g2_out[...] = jnp.concatenate([grad[0:432], grad[432:864]], axis=1)
    w3 = w3_ref[...]
    for plane in range(2):
        u = dot_nn(w3, g2s[plane * 64 : plane * 64 + 192, :])
        back = None
        for b in range(3):
            for c in range(3):
                v = u[(b * 3 + c) * 32 : (b * 3 + c) * 32 + 32]
                if (b, c) != (1, 1):
                    v = rolled(v, -(32 * (1 - b) + (1 - c)))
                    v = jnp.where(keep[1 - b, 1 - c], v, 0.0)
                back = v if back is None else back + v
        back = back * 0.125
        low = 0.3 * back
        for d in range(8):
            at = plane * 256 + d * 32
            g1s[at : at + 32, :] = jnp.where(z1s[at : at + 32, :].astype(F32) > 0, back, low).astype(BF16)
    gram = dot_nt(g1s[0:256, :], px[256:512, :]) + dot_nt(g1s[256:512, :], px[384:640, :])
    total = None
    for d in range(8):
        high, low = split2(gram[d * 32 : d * 32 + 32])
        sel = sel_ref[:, d * 256 : d * 256 + 256]
        term = dot_nt(high, sel) + dot_nt(low, sel)
        total = term if total is None else total + term
    g1_out[...] = total
def compute_kernel(*refs):
    compute(None, lax.axis_index("space"), *refs)


def shift_planes(value, axis, hops):
    count = lax.axis_size(axis)
    return lax.ppermute(value, axis, [(j, j + hops) for j in range(count) if 0 <= j + hops < count])


def local(crop, filter_one, filter_two, cotangent):
    planes = crop[0].reshape(4, 4, 32, 2, 32, 2).transpose(1, 3, 5, 0, 2, 4).reshape(4, 16, LANES)
    cot = cotangent.reshape(64, 256)
    crop14 = jnp.concatenate(
        [
            shift_planes(planes[3:4], "space", 2),
            shift_planes(planes, "space", 1),
            planes,
            shift_planes(planes, "space", -1),
            shift_planes(planes[0:1], "space", -2),
        ]
    )
    cot3 = jnp.stack([shift_planes(cot, "space", 1), cot, shift_planes(cot, "space", -1)])
    sel = jnp.asarray(tap_selection(), BF16)
    taps = jnp.pad(filter_one.reshape(108, 32), ((0, 20), (0, 0)))
    w1 = jnp.einsum("to,tdk->dok", taps, sel.reshape(128, 8, 256), preferred_element_type=F32)
    w1 = w1.astype(BF16).reshape(256, 256)
    f2 = filter_two.reshape(864, 64)
    w2 = f2.T
    w3 = jnp.concatenate([f2[576:864], f2[288:576], f2[0:288]], axis=1)
    feat, two, one = pl.pallas_call(
        compute_kernel,
        out_shape=(
            jax.ShapeDtypeStruct((64, 256), BF16),
            jax.ShapeDtypeStruct((432, 128), F32),
            jax.ShapeDtypeStruct((32, 128), F32),
        ),
        scratch_shapes=[
            pltpu.VMEM((896, LANES), BF16),
            pltpu.VMEM((1728, LANES), BF16),
            pltpu.VMEM((512, LANES), BF16),
            pltpu.VMEM((256, LANES), BF16),
            pltpu.VMEM((512, LANES), BF16),
        ],
        compiler_params=pltpu.CompilerParams(vmem_limit_bytes=60 * 1024 * 1024),
    )(crop14, w1, w2, w3, sel, cot3)
    two, one = lax.psum((two, one), ("dp", "space"))
    two = jnp.concatenate([two[:, 0:64], two[:, 64:128]]).reshape(3, 3, 3, 32, 64)
    one = one.T[0:108].reshape(3, 3, 3, 4, 32)
    return feat.reshape(1, 64, 1, 16, 16), one, two


def solution(mesh):
    placed = (P("dp", None, "space", None, None), P(), P(), P("dp", None, "space", None, None))
    return jax.shard_map(
        local, mesh=mesh, in_specs=placed, out_specs=(P("dp", None, "space", None, None), P(), P()), check_vma=False
    )
```

time: 407 us -> 350 us (0.86); the launches traced: 399 us -> 349 us
  matrix products: 71.1 us -> 0.86 us
  waiting for transfers between devices: 108 us -> 174 us
  local copies, waits for them, and re-layouts: 83.9 us -> 53 us
  other arithmetic: 19.3 us -> 2.21 us
  Pallas kernels: 0 us -> 7.39 us
  blocking collectives: 85.7 us -> 81.4 us
    psum x1, waiting for transfers between devices: 104 us -> 170 us  [local(): two, one = lax.psum((two, one), ('dp', 'space'))]
    dot_general x54 -> x1, matrix products: 37.1 us -> 0.86 us  [local(): jnp.einsum('to,tdk->dok', taps, sel.reshape(128, 8, 256), preferred_eleme...]
    conv_general_dilated x3 -> x0, matrix products: 34 us -> none  [convolve(): lax.conv_general_dilated(source, kernel, (1, 1, 1), ((0, 0), (1, 1), (1,...]
    select_n x6 -> x0, local copies, waits for them, and re-layouts: 33.1 us -> none  [the longest x4 24.2 us: leaky(): return jnp.where(value > 0, value, 0.3 * value)]
    slice x3 -> x8, local copies, waits for them, and re-layouts: 0.82 us -> 33.1 us  [the longest x3 21.3 us: local(): planes[0:1]]
    broadcast_in_dim x6 -> x0, local copies, waits for them, and re-layouts: 17.1 us -> none  [widened(): jnp.broadcast_to(value[:, :, :, None, :, None, :, None], (shape[0], shape...]
    transpose x0 -> x1, local copies, waits for them, and re-layouts: none -> 10.7 us  [local(): crop[0].reshape(4, 4, 32, 2, 32, 2).transpose(1, 3, 5, 0, 2, 4)]
    conv_general_dilated x7 -> x0, local copies, waits for them, and re-layouts: 10.5 us -> none  [convolve(): lax.conv_general_dilated(source, kernel, (1, 1, 1), ((0, 0), (1, 1), (1,...]
  transfers between devices with their start and end apart: 7 -> 7, of which waited for: 3 -> 2; matrix products, arithmetic and copies ran while one was open for 17% -> 11% of each run, Pallas kernels for 0% -> 0%
where the time goes in v1:
time: 350 us; the launch traced here: 349 us
  waiting for transfers between devices  174 us (50%)
  blocking collectives  81.4 us (23%)
  local copies, waits for them, and re-layouts  53 us (15%)
  starting transfers between devices  16.6 us (5%)
  between operations  14.3 us (4%)
  Pallas kernels  7.39 us (2%)
    psum x1, waiting for transfers between devices, local(): two, one = lax.psum((two, one), ('dp', 'space'))  170 us
    psum x1, blocking collectives, local(): two, one = lax.psum((two, one), ('dp', 'space'))  81.4 us
    slice x3, local copies, waits for them, and re-layouts, local(): planes[0:1]  21.3 us
    ppermute x6, starting transfers between devices, shift_planes(): lax.ppermute(value, axis, [(j, j + hops) for j in range(count) if 0 <= j...  16.6 us
    transpose x1, local copies, waits for them, and re-layouts, local(): crop[0].reshape(4, 4, 32, 2, 32, 2).transpose(1, 3, 5, 0, 2, 4)  10.7 us
    slice x2, local copies, waits for them, and re-layouts, local(): planes[3:4]  10.6 us
    pallas_call x1, Pallas kernels, local(): pl.pallas_call(compute_kernel, out_shape=(jax.ShapeDtypeStruct((64, 256),...  7.39 us
  transfers between devices with their start and end apart: 7, of which 2 were waited for; matrix products, arithmetic and copies ran while one was open for 11% of the time, Pallas kernels for 0%

profile of v1, /device:TPU:1, one launch (start us, length us, event | category | flops | bytes accessed | tf_op | source)
XLA Modules:
  0.0 349.3 jit_solution(18334718482658993519)
XLA Ops:
  7.2 0.0 copy-start.3
  7.2 0.0 all-reduce.3.cloned.1.call-start
  7.2 4.6 %copy.15 = bf16[1,4,4,64,64]{2,4,3,1,0:T(8,128)(2,1)} copy(bf16[1,4,4,64,64]{4,3,2,1,0:T(8,128)(2,1)} %param.5) | data formatting | bytes 262144 | tf_op args[0]
  11.8 10.7 %copy.17 = bf16[4,2,2,4,32,32]{5,4,3,2,1,0:T(8,128)(2,1)S(1)} copy(bf16[4,2,2,4,32,32]{0,2,5,1,4,3:T(2,128)(2,1)} %bitcast.29) | data formatting | bytes 262144 | tf_op jit(solution)/shard_map/transpose | solution.py:171
  22.5 0.5 reshape.38
  23.1 4.6 %collective-permute-start.1 = (bf16[4,16,1024]{2,1,0:T(8,128)(2,1)S(1)}, bf16[4,16,1024]{2,1,0:T(8,128)(2,1)S(1)}, u32[]{:S(2)}, u32[]{:S(2)}) collective-permute-start(bf16[4,16,1024]{2,1,0:T(8,128)(2,1)S(1)} %reshape.38), channel_id=1, source_target_pairs={{0,1},{1,2},{2,3},{3,4},{4,5},{5,6},{6,7},{7,8},{8,9},{9,10},{10,1... | collective-permute-start | bytes 393224 | tf_op jit(solution)/shard_map/ppermute | solution.py:167
  27.7 1.9 collective-permute-start.2
  29.6 0.0 copy-done.3
  29.6 0.1 copy.21
  29.7 1.9 collective-permute-start.5
  31.6 3.6 %collective-permute-start.4 = (bf16[64,256]{1,0:T(8,128)(2,1)S(1)}, bf16[64,256]{1,0:T(8,128)(2,1)S(1)}, u32[]{:S(2)}, u32[]{:S(2)}) collective-permute-start(bf16[64,256]{1,0:T(8,128)(2,1)S(1)} %copy.21), channel_id=1, source_target_pairs={{0,1},{1,2},{2,3},{3,4},{4,5},{5,6},{6,7},{7,8},{8,9},{9,10},{10,1... | collective-permute-start | bytes 98312 | tf_op jit(solution)/shard_map/ppermute | solution.py:167
  35.3 10.8 %fusion.1 = (bf16[1,2,2,4,32,32]{0,2,5,1,4,3:T(2,128)(2,1)}, bf16[1,2,2,4,32,32]{0,2,5,1,4,3:T(2,128)(2,1)}) fusion(bf16[4,2,2,4,32,32]{0,2,5,1,4,3:T(2,128)(2,1)} %bitcast.30), kind=kLoop, calls=%fused_computation.11 | loop fusion | bytes 131072 | tf_op jit(solution)/shard_map/slice | solution.py:179
  46.1 0.0 copy-start.4
  46.1 0.0 copy-start
  46.1 0.0 copy-start.2
  46.1 10.4 %copy.16 = bf16[1,2,2,4,32,32]{5,4,3,2,1,0:T(8,128)(2,1)S(1)} copy(bf16[1,2,2,4,32,32]{0,2,5,1,4,3:T(2,128)(2,1)} %get-tuple-element.13) | data formatting | bytes 65536 | tf_op jit(solution)/shard_map/slice | solution.py:175
  56.5 0.2 slice.40
  56.7 3.2 collective-permute-start
  59.9 0.0 copy-done.4
  59.9 0.1 copy.19
  60.0 0.0 copy-done
  60.0 0.0 copy-done.2
  60.0 0.9 convolution_convert_fusion
  60.9 0.8 pad_maximum_fusion.1.refs_3_
  61.7 10.3 %copy.18 = bf16[1,2,2,4,32,32]{5,4,3,2,1,0:T(8,128)(2,1)S(1)} copy(bf16[1,2,2,4,32,32]{0,2,5,1,4,3:T(2,128)(2,1)} %get-tuple-element.12) | data formatting | bytes 65536 | tf_op jit(solution)/shard_map/slice | solution.py:179
  72.0 0.2 slice.42
  72.1 0.8 copy.20
  72.9 0.1 copy.23
  73.0 0.0 collective-permute-done
  73.0 1.3 collective-permute-start.3
  74.3 0.0 collective-permute-done.5
  74.3 0.0 collective-permute-done.4
  74.3 0.6 pad_maximum_fusion.2.refs_5_
  75.0 0.0 collective-permute-done.1
  75.0 0.0 collective-permute-done.2
  75.1 3.2 collective-permute-done.3
  78.3 0.0 copy-start.1
  78.3 0.8 copy-done.1
  79.1 7.4 %shard_map.76 = (bf16[64,256]{1,0:T(8,128)(2,1)}, f32[432,128]{1,0:T(8,128)}, f32[32,128]{1,0:T(8,128)}) custom-call(bf16[14,16,1024]{2,1,0:T(8,128)(2,1)} %copy-done.1, bf16[256,256]{1,0:T(8,128)(2,1)} %bitcast.32, bf16[64,864]{1,0:T(8,128)(2,1)} %bitcast.33, bf16[288,192]{1,0:T(8,128)(2,1)} %pad_maximum_fusion.1.refs_3_, ...), custom_call_target="tpu_custom_call" | custom-call | tf_op jit(solution)/shard_map/pallas_call | solution.py:190
  86.4 0.0 all-reduce.3.cloned.1.call-update
  86.5 1.5 copy.24
  88.0 81.4 %psum.14 = f32[128,32]{0,1:T(8,128)S(1)} all-reduce(f32[128,32]{0,1:T(8,128)} %bitcast.44), channel_id=1, replica_groups=mesh['dp'=8,'space'=32] {'dp','space'}, use_global_device_ids=true, to_apply=%region_0.1 | all-reduce | flops 4096 | bytes 32768 | tf_op jit(solution)/shard_map/psum | solution.py:206
  169.4 0.1 copy.25
  169.5 0.6 reshape.45
  170.1 170.3 %all-reduce.3.cloned.1.call-done = f32[432,128]{1,0:T(8,128)} async-done(((f32[432,128]{1,0:T(8,128)}), f32[432,128]{1,0:T(8,128)}) %all-reduce.3.cloned.1.call-update) | async-done | bytes 221200 | tf_op jit(solution)/shard_map/psum | solution.py:206
  340.5 1.2 fusion.2
  341.6 0.8 pad_maximum_fusion
  (7 shorter events, 0.1 us)
Async XLA Ops:
  7.2 22.4 %copy-start.3 = (bf16[1,64,1,16,16]{1,4,3,2,0:T(8,128)(2,1)S(1)}, bf16[1,64,1,16,16]{1,4,3,2,0:T(8,128)(2,1)}, u32[]{:S(2)}) copy-start(bf16[1,64,1,16,16]{1,4,3,2,0:T(8,128)(2,1)} %param.8) | copy-start | bytes 98308
  7.2 333.3 %all-reduce.3.cloned.1.call-start = ((), (), s32[]{:S(2)}) async-start(), calls=%async_computation | async-start | bytes 442368 | tf_op jit(solution)/shard_map/psum | solution.py:206
  23.1 51.9 %collective-permute-start.1 = (bf16[4,16,1024]{2,1,0:T(8,128)(2,1)S(1)}, bf16[4,16,1024]{2,1,0:T(8,128)(2,1)S(1)}, u32[]{:S(2)}, u32[]{:S(2)}) collective-permute-start(bf16[4,16,1024]{2,1,0:T(8,128)(2,1)S(1)} %reshape.38), channel_id=1, source_target_pairs={{0,1},{1,2},{2,3},{3,4},{4,5},{5,6},{6,7},{7,8},{8,9},{9,10},{10,1... | collective-permute-start | bytes 393224 | tf_op jit(solution)/shard_map/ppermute | solution.py:167
  27.7 47.4 %collective-permute-start.2 = (bf16[4,16,1024]{2,1,0:T(8,128)(2,1)S(1)}, bf16[4,16,1024]{2,1,0:T(8,128)(2,1)S(1)}, u32[]{:S(2)}, u32[]{:S(2)}) collective-permute-start(bf16[4,16,1024]{2,1,0:T(8,128)(2,1)S(1)} %reshape.38), channel_id=1, source_target_pairs={{1,0},{2,1},{3,2},{4,3},{5,4},{6,5},{7,6},{8,7},{9,8},{10,9},{11,1... | collective-permute-start | bytes 393224 | tf_op jit(solution)/shard_map/ppermute | solution.py:167
  29.7 44.6 %collective-permute-start.5 = (bf16[64,256]{1,0:T(8,128)(2,1)S(1)}, bf16[64,256]{1,0:T(8,128)(2,1)S(1)}, u32[]{:S(2)}, u32[]{:S(2)}) collective-permute-start(bf16[64,256]{1,0:T(8,128)(2,1)S(1)} %copy.21), channel_id=1, source_target_pairs={{1,0},{2,1},{3,2},{4,3},{5,4},{6,5},{7,6},{8,7},{9,8},{10,9},{11,1... | collective-permute-start | bytes 98312 | tf_op jit(solution)/shard_map/ppermute | solution.py:167
  31.6 42.7 %collective-permute-start.4 = (bf16[64,256]{1,0:T(8,128)(2,1)S(1)}, bf16[64,256]{1,0:T(8,128)(2,1)S(1)}, u32[]{:S(2)}, u32[]{:S(2)}) collective-permute-start(bf16[64,256]{1,0:T(8,128)(2,1)S(1)} %copy.21), channel_id=1, source_target_pairs={{0,1},{1,2},{2,3},{3,4},{4,5},{5,6},{6,7},{7,8},{8,9},{9,10},{10,1... | collective-permute-start | bytes 98312 | tf_op jit(solution)/shard_map/ppermute | solution.py:167
  46.1 13.8 %copy-start.4 = (bf16[3,3,3,4,32]{4,3,2,1,0:T(4,128)(2,1)S(1)}, bf16[3,3,3,4,32]{4,3,2,1,0:T(4,128)(2,1)}, u32[]{:S(2)}) copy-start(bf16[3,3,3,4,32]{4,3,2,1,0:T(4,128)(2,1)} %param.6) | copy-start | bytes 20740
  46.1 13.9 %copy-start = (bf16[3,3,3,32,64]{4,3,2,1,0:T(8,128)(2,1)S(1)}, bf16[3,3,3,32,64]{4,3,2,1,0:T(8,128)(2,1)}, u32[]{:S(2)}) copy-start(bf16[3,3,3,32,64]{4,3,2,1,0:T(8,128)(2,1)} %param.7) | copy-start | bytes 331780
  46.1 13.9 %copy-start.2 = (bf16[128,8,256]{2,0,1:T(8,128)(2,1)S(1)}, bf16[128,8,256]{2,0,1:T(8,128)(2,1)}, u32[]{:S(2)}) copy-start(bf16[128,8,256]{2,0,1:T(8,128)(2,1)} %constant.10) | copy-start | bytes 1572868
  56.7 16.3 %collective-permute-start = (bf16[1,16,1024]{2,1,0:T(8,128)(2,1)S(1)}, bf16[1,16,1024]{2,1,0:T(8,128)(2,1)S(1)}, u32[]{:S(2)}, u32[]{:S(2)}) collective-permute-start(bf16[1,16,1024]{2,1,0:T(8,128)(2,1)S(1)} %slice.40), channel_id=1, source_target_pairs={{0,2},{1,3},{2,4},{3,5},{4,6},{5,7},{6,8},{7,9},{8,10},{9,11},{10,... | collective-permute-start | bytes 98312 | tf_op jit(solution)/shard_map/ppermute | solution.py:167
  73.0 5.2 %collective-permute-start.3 = (bf16[1,16,1024]{2,1,0:T(8,128)(2,1)S(1)}, bf16[1,16,1024]{2,1,0:T(8,128)(2,1)S(1)}, u32[]{:S(2)}, u32[]{:S(2)}) collective-permute-start(bf16[1,16,1024]{2,1,0:T(8,128)(2,1)S(1)} %slice.42), channel_id=1, source_target_pairs={{2,0},{3,1},{4,2},{5,3},{6,4},{7,5},{8,6},{9,7},{10,8},{11,9},{12,... | collective-permute-start | bytes 98312 | tf_op jit(solution)/shard_map/ppermute | solution.py:167
  78.3 0.8 copy-start.1
Sparse Core Ops, SparseCore 0:
  86.6 253.8 all-reduce.2

commit v2 on v1

--- a/solution.py
+++ b/solution.py
@@ -158,28 +158,219 @@
         term = dot_nt(high, sel) + dot_nt(low, sel)
         total = term if total is None else total + term
     g1_out[...] = total
-def compute_kernel(*refs):
-    compute(None, lax.axis_index("space"), *refs)
-
-
-def shift_planes(value, axis, hops):
-    count = lax.axis_size(axis)
-    return lax.ppermute(value, axis, [(j, j + hops) for j in range(count) if 0 <= j + hops < count])
+
+
+NX, NY, NZH, NZL = 4, 4, 2, 4
+ROWS = 16
+
+
+class Place:
+    def __init__(self):
+        dp, self.s = lax.axis_index("dp"), lax.axis_index("space")
+        self.zh, self.x = dp // NX, dp % NX
+        self.core = self.s % 2
+        self.y = self.s // 2 % NY
+        self.zl = self.s // 2 // NY
+        self.z = self.zh * NZL + self.zl
+
+    def at(self, x, y, z, core):
+        return {"dp": z // NZL * NX + x, "space": (z % NZL * NY + y) * 2 + core}
+
+    def plane_peer(self, dx, dy):
+        x, y = (self.x + dx) % NX, (self.y + dy) % NY
+        return self.at(x, y, self.z, self.core), x * NY + y
+
+    def depth_peer(self, dz):
+        return self.at(self.x, self.y, (self.z + dz) % (NZH * NZL), self.core)
+
+    def partner(self):
+        return self.at(self.x, self.y, self.z, 1 - self.core)
+
+
+def ring_order(count):
+    return sorted(range(count), key=lambda d: -min(d, count - d))
+
+
+def plane_offsets():
+    far = lambda d: min(d[0], NX - d[0]) + min(d[1], NY - d[1])
+    every = [(dx, dy) for dx in range(NX) for dy in range(NY)]
+    return sorted(every, key=lambda d: -far(d))
+
+
+def remote(src, dst, send, recv, peer):
+    return pltpu.make_async_remote_copy(
+        src_ref=src, dst_ref=dst, send_sem=send, recv_sem=recv, device_id=peer, device_id_type=pl.DeviceIdType.MESH
+    )
+
+
+HALO_HOPS = (1, -1, 2, -2)
+
+
+def greet(place, with_halo):
+    barrier = pltpu.get_barrier_semaphore()
+    peers = [place.partner()]
+    peers += [place.plane_peer(dx, dy)[0] for dx, dy in plane_offsets()[:-1]]
+    peers += [place.depth_peer(d) for d in range(1, NZH * NZL)]
+    if with_halo:
+        count = lax.axis_size("space")
+        peers += [{"space": (place.s + hop + count) % count} for hop in HALO_HOPS]
+    for peer in peers:
+        pl.semaphore_signal(barrier, inc=1, device_id=peer, device_id_type=pl.DeviceIdType.MESH)
+    return lambda: pl.semaphore_wait(barrier, len(peers))
+
+
+class Halo:
+    def __init__(self, place, own_ref, cot_ref, wide, cots, send, recv):
+        self.s, self.count = place.s, lax.axis_size("space")
+        moves = (
+            (1, own_ref, wide.at[1:5]),
+            (-1, own_ref, wide.at[9:13]),
+            (2, own_ref.at[3:4], wide.at[0:1]),
+            (-2, own_ref.at[0:1], wide.at[13:14]),
+            (1, cot_ref, cots.at[0]),
+            (-1, cot_ref, cots.at[2]),
+        )
+        self.items = []
+        for k, (hop, src, dst) in enumerate(moves):
+            peer = {"space": (self.s + hop + self.count) % self.count}
+            self.items.append((hop, dst, remote(src, dst, send.at[k], recv.at[k], peer)))
+
+    def exists(self, hop):
+        there = self.s + hop
+        return (there >= 0) & (there < self.count)
+
+    def start(self):
+        for hop, dst, copy in self.items:
+            pl.when(self.exists(hop))(copy.start)
+
+            @pl.when(jnp.logical_not(self.exists(-hop)))
+            def _():
+                dst[...] = jnp.zeros(dst.shape, BF16)
+
+    def wait(self):
+        for hop, dst, copy in self.items:
+            pl.when(self.exists(-hop))(copy.wait_recv)
+
+    def drain(self):
+        for hop, dst, copy in self.items:
+            pl.when(self.exists(hop))(copy.wait_send)
+
+
+def all_reduce(place, acc, r0, s0, r1, r2, fin, sems):
+    send0, recv0, send1, recv1, send2, recv2, send3, recv3, send4, recv4 = sems
+    half = NX * NY * ROWS
+    offsets = plane_offsets()
+    last = len(offsets) - 1
+    mine = place.core * half
+    other = half - mine
+
+    def rows(start):
+        return pl.ds(pl.multiple_of(start, ROWS), ROWS)
+
+    partner = place.partner()
+    sent = []
+    chunk = [place.plane_peer(dx, dy) for dx, dy in offsets]
+    arrive0 = []
+    for k, (_, j) in enumerate(chunk):
+        copy = remote(acc.at[rows(other + j * ROWS)], r0.at[rows(j * ROWS)], send0.at[k], recv0.at[k], partner)
+        copy.start()
+        arrive0.append(copy)
+    sent += arrive0
+    arrive1 = []
+
+    def pass_on(k):
+        peer, j = chunk[k]
+        copy = remote(s0.at[rows(j * ROWS)], r1.at[k], send1.at[k], recv1.at[k], peer)
+        copy.start()
+        arrive1.append(copy)
+
+    for k, (peer, j) in enumerate(chunk):
+        arrive0[k].wait_recv()
+        s0[rows(j * ROWS), :] = acc[rows(mine + j * ROWS), :] + r0[rows(j * ROWS), :]
+        if k >= 1:
+            pass_on(k - 1)
+    sent += arrive1
+    own = chunk[last][1]
+    total = s0[rows(own * ROWS), :]
+    for k in range(last - 1, -1, -1):
+        arrive1[k].wait_recv()
+        total = total + r1[k]
+    r2[place.z] = total
+    arrive2 = []
+    depth = NZH * NZL
+    for k, d in enumerate(ring_order(depth)[:-1]):
+        copy = remote(r2.at[place.z], r2.at[place.z], send2.at[k], recv2.at[k], place.depth_peer(d))
+        copy.start()
+        arrive2.append(copy)
+    sent += arrive2
+    for copy in arrive2:
+        copy.wait_recv()
+    total = r2[0]
+    for z in range(1, depth):
+        total = total + r2[z]
+    at_own = rows(mine + own * ROWS)
+    fin[at_own, :] = total
+    arrive3 = []
+    for k in range(last):
+        copy = remote(fin.at[at_own], fin.at[at_own], send3.at[k], recv3.at[k], chunk[k][0])
+        copy.start()
+        arrive3.append(copy)
+    sent += arrive3
+
+    def hand_over(k, start):
+        at = rows(mine + start * ROWS)
+        copy = remote(fin.at[at], fin.at[at], send4.at[k], recv4.at[k], partner)
+        copy.start()
+        return copy
+
+    arrive4 = [hand_over(last, own)]
+    for k in range(last - 1, -1, -1):
+        arrive3[k].wait_recv()
+        dx, dy = offsets[k]
+        source = (place.x - dx + NX) % NX * NY + (place.y - dy + NY) % NY
+        arrive4.append(hand_over(k, source))
+    for copy in arrive4:
+        copy.wait_recv()
+    return sent + arrive4
+
+
+def reduce_scratch():
+    half = NX * NY * ROWS
+    n, depth = NX * NY, NZH * NZL
+    dma = pltpu.SemaphoreType.DMA
+    return [
+        pltpu.VMEM((2 * half, 128), F32),
+        pltpu.VMEM((half, 128), F32),
+        pltpu.VMEM((half, 128), F32),
+        pltpu.VMEM((n, ROWS, 128), F32),
+        pltpu.VMEM((depth, ROWS, 128), F32),
+        pltpu.VMEM((2 * half, 128), F32),
+    ], [dma((n,)), dma((n,)), dma((n,)), dma((n,)), dma((depth,)), dma((depth,)), dma((n,)), dma((n,)), dma((n,)), dma((n,))]
+
+
+def whole_kernel(crop_ref, w1_ref, w2_ref, w3_ref, sel_ref, cot_ref, feat_ref, sum_ref, wide, cots, px, maps, z1s, g2s, g1s,
+                 acc, r0, s0, r1, r2, fin, halo_send, halo_recv, *sems):
+    place = Place()
+    ready = greet(place, True)
+    wide[5:9] = crop_ref[...]
+    cots[1] = cot_ref[...]
+    acc[464:512, :] = jnp.zeros((48, 128), F32)
+    halo = Halo(place, crop_ref, cot_ref, wide, cots, halo_send, halo_recv)
+    ready()
+    halo.start()
+    halo.wait()
+    compute(None, place.s, wide, w1_ref, w2_ref, w3_ref, sel_ref, cots, feat_ref, acc.at[0:432], acc.at[432:464],
+            px, maps, z1s, g2s, g1s)
+    sent = all_reduce(place, acc, r0, s0, r1, r2, fin, sems)
+    sum_ref[...] = fin[...]
+    halo.drain()
+    for copy in sent:
+        copy.wait_send()
 
 
 def local(crop, filter_one, filter_two, cotangent):
     planes = crop[0].reshape(4, 4, 32, 2, 32, 2).transpose(1, 3, 5, 0, 2, 4).reshape(4, 16, LANES)
     cot = cotangent.reshape(64, 256)
-    crop14 = jnp.concatenate(
-        [
-            shift_planes(planes[3:4], "space", 2),
-            shift_planes(planes, "space", 1),
-            planes,
-            shift_planes(planes, "space", -1),
-            shift_planes(planes[0:1], "space", -2),
-        ]
-    )
-    cot3 = jnp.stack([shift_planes(cot, "space", 1), cot, shift_planes(cot, "space", -1)])
     sel = jnp.asarray(tap_selection(), BF16)
     taps = jnp.pad(filter_one.reshape(108, 32), ((0, 20), (0, 0)))
     w1 = jnp.einsum("to,tdk->dok", taps, sel.reshape(128, 8, 256), preferred_element_type=F32)
@@ -187,25 +378,29 @@
     f2 = filter_two.reshape(864, 64)
     w2 = f2.T
     w3 = jnp.concatenate([f2[576:864], f2[288:576], f2[0:288]], axis=1)
-    feat, two, one = pl.pallas_call(
-        compute_kernel,
-        out_shape=(
-            jax.ShapeDtypeStruct((64, 256), BF16),
-            jax.ShapeDtypeStruct((432, 128), F32),
-            jax.ShapeDtypeStruct((32, 128), F32),
-        ),
+    buffers, sems = reduce_scratch()
+    feat, sums = pl.pallas_call(
+        whole_kernel,
+        out_shape=(jax.ShapeDtypeStruct((64, 256), BF16), jax.ShapeDtypeStruct((512, 128), F32)),
         scratch_shapes=[
+            pltpu.VMEM((14, 16, LANES), BF16),
+            pltpu.VMEM((3, 64, 256), BF16),
             pltpu.VMEM((896, LANES), BF16),
             pltpu.VMEM((1728, LANES), BF16),
             pltpu.VMEM((512, LANES), BF16),
             pltpu.VMEM((256, LANES), BF16),
             pltpu.VMEM((512, LANES), BF16),
+            *buffers,
+            pltpu.SemaphoreType.DMA((6,)),
+            pltpu.SemaphoreType.DMA((6,)),
+            *sems,
         ],
-        compiler_params=pltpu.CompilerParams(vmem_limit_bytes=60 * 1024 * 1024),
-    )(crop14, w1, w2, w3, sel, cot3)
-    two, one = lax.psum((two, one), ("dp", "space"))
-    two = jnp.concatenate([two[:, 0:64], two[:, 64:128]]).reshape(3, 3, 3, 32, 64)
-    one = one.T[0:108].reshape(3, 3, 3, 4, 32)
+        compiler_params=pltpu.CompilerParams(
+            vmem_limit_bytes=60 * 1024 * 1024, collective_id=0, has_side_effects=True
+        ),
+    )(planes, w1, w2, w3, sel, cot)
+    two = jnp.concatenate([sums[0:432, 0:64], sums[0:432, 64:128]]).reshape(3, 3, 3, 32, 64)
+    one = sums[432:464].T[0:108].reshape(3, 3, 3, 4, 32)
     return feat.reshape(1, 64, 1, 16, 16), one, two
 
 

time: 350 us -> 67.3 us (0.19)
  waiting for transfers between devices: 174 us -> 0 us
  blocking collectives: 81.4 us -> 0 us
  Pallas kernels: 7.39 us -> 41.4 us
  local copies, waits for them, and re-layouts: 53 us -> 22.3 us
  starting transfers between devices: 16.6 us -> 0 us
  between operations: 14.3 us -> 0.69 us
    psum x1 -> x0, waiting for transfers between devices: 170 us -> none  [local(): two, one = lax.psum((two, one), ('dp', 'space'))]
    psum x1 -> x0, blocking collectives: 81.4 us -> none  [local(): two, one = lax.psum((two, one), ('dp', 'space'))]
    pallas_call x1, Pallas kernels: 7.39 us -> 41.4 us  [local(): pl.pallas_call(whole_kernel, out_shape=(jax.ShapeDtypeStruct((64, 256), B...]
    slice x7 -> x2, local copies, waits for them, and re-layouts: 33.1 us -> 1.26 us  [the longest x1 1.15 us: local(): sums[0:432, 0:64]]
    ppermute x6 -> x0, starting transfers between devices: 16.6 us -> none  [shift_planes(): lax.ppermute(value, axis, [(j, j + hops) for j in range(count) if 0 <= j...]
  transfers between devices with their start and end apart: 7 -> 0, of which waited for: 2 -> 0; matrix products, arithmetic and copies ran while one was open for 11% -> 0% of each run, Pallas kernels for 0% -> 0%
where the time goes in v2:
time: 67.3 us; the launch traced here: 66.8 us
  Pallas kernels  41.4 us (62%)
  local copies, waits for them, and re-layouts  22.3 us (33%)
  other arithmetic  1.57 us (2%)
  matrix products  0.87 us (1%)
  between operations  0.69 us (1%)
    pallas_call x1, Pallas kernels, local(): pl.pallas_call(whole_kernel, out_shape=(jax.ShapeDtypeStruct((64, 256), B...  41.4 us
    transpose x1, local copies, waits for them, and re-layouts, local(): crop[0].reshape(4, 4, 32, 2, 32, 2).transpose(1, 3, 5, 0, 2, 4)  10.7 us
    unnamed x9, local copies, waits for them, and re-layouts  4.68 us
    pallas_call x1, local copies, waits for them, and re-layouts, local(): pl.pallas_call(whole_kernel, out_shape=(jax.ShapeDtypeStruct((64, 256), B...  1.49 us

profile of v2, /device:TPU:1, one launch (start us, length us, event | category | flops | bytes accessed | tf_op | source)
XLA Modules:
  0.0 66.8 jit_solution(7656329632763080514)
XLA Ops:
  0.6 0.0 copy-start.1
  0.6 0.0 copy-start.3
  0.7 0.0 copy-start
  0.7 4.7 %copy.14 = bf16[1,4,4,64,64]{2,4,3,1,0:T(8,128)(2,1)} copy(bf16[1,4,4,64,64]{4,3,2,1,0:T(8,128)(2,1)} %param.5) | data formatting | bytes 262144 | tf_op args[0]
  5.3 0.0 copy-start.2
  5.3 10.7 %copy.15 = bf16[4,2,2,4,32,32]{5,4,3,2,1,0:T(8,128)(2,1)S(1)} copy(bf16[4,2,2,4,32,32]{0,2,5,1,4,3:T(2,128)(2,1)} %bitcast.23) | data formatting | bytes 262144 | tf_op jit(solution)/shard_map/transpose | solution.py:372
  16.0 1.2 %reshape.36.crop_ref = bf16[4,16,1024]{2,1,0:T(8,128)(2,1)} reshape(bf16[4,2,2,4,32,32]{5,4,3,2,1,0:T(8,128)(2,1)S(1)} %copy.15) | data formatting | bytes 262144 | tf_op jit(solution)/shard_map/reshape | solution.py:372
  17.2 0.0 copy-done.3
  17.3 0.1 copy.16
  17.3 0.0 copy-done.1
  17.3 0.9 %convolution_convert_fusion = bf16[32,8,256]{2,0,1:T(8,128)(2,1)} fusion(bf16[128,8,256]{2,0,1:T(8,128)(2,1)S(1)} %copy-done.1, bf16[108,32]{0,1:T(8,128)(2,1)S(1)} %copy.16), kind=kOutput, calls=%fused_computation | convolution fusion | flops 16842752 | bytes 662272 | tf_op jit(solution)/shard_map/to,tdk->dok/dot_general | solution.py:376
  18.2 0.0 copy-done
  18.2 0.8 %copy.17 = bf16[864,64]{0,1:T(8,128)(2,1)} copy(bf16[864,64]{1,0:T(8,128)(2,1)S(1)} %bitcast.24) | data formatting | bytes 221184 | tf_op jit(solution)/shard_map/reshape | solution.py:378
  19.0 0.8 %pad_maximum_fusion.1.w3_ref = bf16[288,192]{1,0:T(8,128)(2,1)} fusion(bf16[288,64]{1,0:T(8,128)(2,1)S(1)} %bitcast.29, bf16[288,64]{1,0:T(8,128)(2,1)S(1)} %bitcast.30, bf16[288,64]{1,0:T(8,128)(2,1)S(1)} %bitcast.28), kind=kLoop, calls=%fused_computation.2 | loop fusion | flops 331776 | bytes 221184 | tf_op jit(solution)/shard_map/concatenate | solution.py:380
  19.8 0.0 copy-done.2
  19.8 0.7 %copy.18.cot_ref = bf16[64,256]{1,0:T(8,128)(2,1)} copy(bf16[64,256]{0,1:T(8,128)(2,1)S(1)} %bitcast.31) | data formatting | bytes 65536 | tf_op jit(solution)/shard_map/reshape | solution.py:373
  20.5 41.4 %shard_map.76 = (bf16[64,256]{1,0:T(8,128)(2,1)}, f32[512,128]{1,0:T(8,128)}) custom-call(bf16[4,16,1024]{2,1,0:T(8,128)(2,1)} %reshape.36.crop_ref, bf16[256,256]{1,0:T(8,128)(2,1)} %bitcast.25, bf16[64,864]{1,0:T(8,128)(2,1)} %bitcast.26, bf16[288,192]{1,0:T(8,128)(2,1)} %pad_maximum_fusion.1.w3_ref, bf16[128,2048]{1,0:T(8,128)(2,1)} %constant.5.clone.sel_ref, ...), custom_call_target="tpu_custom_call" | custom-call | tf_op jit(solution)/shard_map/pallas_call | solution.py:382
  61.9 1.5 %copy.19 = bf16[64,256]{0,1:T(8,128)(2,1)} copy(bf16[64,256]{1,0:T(8,128)(2,1)} %get-tuple-element.5) | data formatting | bytes 65536 | tf_op jit(solution)/shard_map/pallas_call | solution.py:382
  63.4 0.7 %slice_bitcast_fusion = f32[128,32]{0,1:T(8,128)S(1)} fusion(f32[512,128]{1,0:T(8,128)} %get-tuple-element.6), kind=kLoop, calls=%fused_computation.3 | loop fusion | bytes 32768 | tf_op jit(solution)/shard_map/transpose | solution.py:403
  64.1 0.1 copy.20
  64.2 0.6 reshape.43
  64.8 1.2 %fusion.1 = (f32[432,64]{1,0:T(8,128)S(1)}, f32[432,64]{1,0:T(8,128)S(1)}) fusion(f32[512,128]{1,0:T(8,128)} %get-tuple-element.6), kind=kLoop, calls=%fused_computation.6 | loop fusion | bytes 442368 | tf_op jit(solution)/shard_map/slice | solution.py:402
  66.0 0.8 %pad_maximum_fusion = f32[864,64]{1,0:T(8,128)} fusion(f32[432,64]{1,0:T(8,128)S(1)} %get-tuple-element.11, f32[432,64]{1,0:T(8,128)S(1)} %get-tuple-element.10), kind=kLoop, calls=%fused_computation.1 | loop fusion | flops 55296 | bytes 442368 | tf_op jit(solution)/shard_map/concatenate | solution.py:402
  (2 shorter events, 0.0 us)
Async XLA Ops:
  0.6 16.7 %copy-start.1 = (bf16[128,8,256]{2,0,1:T(8,128)(2,1)S(1)}, bf16[128,8,256]{2,0,1:T(8,128)(2,1)}, u32[]{:S(2)}) copy-start(bf16[128,8,256]{2,0,1:T(8,128)(2,1)} %constant.10) | copy-start | bytes 1572868
  0.6 16.6 %copy-start.3 = (bf16[3,3,3,4,32]{4,3,2,1,0:T(4,128)(2,1)S(1)}, bf16[3,3,3,4,32]{4,3,2,1,0:T(4,128)(2,1)}, u32[]{:S(2)}) copy-start(bf16[3,3,3,4,32]{4,3,2,1,0:T(4,128)(2,1)} %param.6) | copy-start | bytes 20740
  0.7 17.6 %copy-start = (bf16[3,3,3,32,64]{4,3,2,1,0:T(8,128)(2,1)S(1)}, bf16[3,3,3,32,64]{4,3,2,1,0:T(8,128)(2,1)}, u32[]{:S(2)}) copy-start(bf16[3,3,3,32,64]{4,3,2,1,0:T(8,128)(2,1)} %param.7) | copy-start | bytes 331780
  5.3 14.5 %copy-start.2 = (bf16[1,64,1,16,16]{1,4,3,2,0:T(8,128)(2,1)S(1)}, bf16[1,64,1,16,16]{1,4,3,2,0:T(8,128)(2,1)}, u32[]{:S(2)}) copy-start(bf16[1,64,1,16,16]{1,4,3,2,0:T(8,128)(2,1)} %param.8) | copy-start | bytes 98308

commit v3 on v2

--- a/solution.py
+++ b/solution.py
@@ -130,7 +130,7 @@
                 lanes = slice(256 * j, 256 * j + 256)
                 feat_ref[:, 64 * j : 64 * j + 64] = (
                     (dot_nn(high[:, lanes], gather) + dot_nn(low[:, lanes], gather)) * 0.125
-                ).astype(BF16)
+                )
     grad = dot_nt(maps[288 : 288 + 864, :], g2s[64:128, :])
     grad = grad + dot_nt(maps[576 : 576 + 864, :], g2s[128:192, :])
     g2_out[...] = jnp.concatenate([grad[0:432], grad[432:864]], axis=1)
@@ -348,40 +348,73 @@
     ], [dma((n,)), dma((n,)), dma((n,)), dma((n,)), dma((depth,)), dma((depth,)), dma((n,)), dma((n,)), dma((n,)), dma((n,))]
 
 
-def whole_kernel(crop_ref, w1_ref, w2_ref, w3_ref, sel_ref, cot_ref, feat_ref, sum_ref, wide, cots, px, maps, z1s, g2s, g1s,
-                 acc, r0, s0, r1, r2, fin, halo_send, halo_recv, *sems):
+def iota2(shape):
+    return lax.broadcasted_iota(jnp.int32, shape, 0), lax.broadcasted_iota(jnp.int32, shape, 1)
+
+
+def flatten_planes(crop_ref, wide, cf, lp, fs):
+    cf[...] = crop_ref[...].astype(F32)
+    for h in range(32):
+        pair = [cf[pl.ds(2 * h + e, 16, stride=64), :] for e in range(2)]
+        lp[h // 4 * 16 : h // 4 * 16 + 16, h % 4 * 128 : h % 4 * 128 + 128] = jnp.concatenate(pair, axis=1).astype(BF16)
+    k, n = iota2((512, 512))
+    to = (k // 64 % 2 * 2 + k % 2) * 128 + k // 128 * 32 + k % 64 // 2
+    moved = dot_nn(lp[...], ones(to == n))
+    for block in range(8):
+        for c in range(4):
+            fs[16 * c : 16 * c + 16, 128 * block : 128 * block + 128] = moved[
+                16 * block : 16 * block + 16, 128 * c : 128 * c + 128
+            ].astype(BF16)
+    m, n = iota2((64, 64))
+    rows = dot_nn(ones(m // 4 % 4 * 16 + m % 4 * 4 + m // 16 == n), fs[...])
+    for p in range(4):
+        wide[5 + p] = rows[16 * p : 16 * p + 16].astype(BF16)
+
+
+def whole_kernel(crop_ref, f1_ref, f2_ref, sel_ref, cot_ref, feat_ref, one_ref, two_ref, wide, cots, px, maps, z1s, g2s, g1s,
+                 cf, lp, fs, f1s, w1s, w2s, w3s, feats, acc, r0, s0, r1, r2, fin, halo_send, halo_recv, *sems):
     place = Place()
     ready = greet(place, True)
-    wide[5:9] = crop_ref[...]
-    cots[1] = cot_ref[...]
-    acc[464:512, :] = jnp.zeros((48, 128), F32)
-    halo = Halo(place, crop_ref, cot_ref, wide, cots, halo_send, halo_recv)
+    flatten_planes(crop_ref, wide, cf, lp, fs)
+    cots[1] = cot_ref[...].astype(F32).T.astype(BF16)
+    halo = Halo(place, wide.at[5:9], cots.at[1], wide, cots, halo_send, halo_recv)
     ready()
     halo.start()
+    f1s[108:128, :] = jnp.zeros((20, 32), F32)
+    for t in range(27):
+        f1s[4 * t : 4 * t + 4, :] = f1_ref[t].astype(F32)
+    w1 = dot_nn(f1s[...].T.astype(BF16), sel_ref[...]).astype(BF16)
+    for d in range(8):
+        w1s[32 * d : 32 * d + 32, :] = w1[:, 256 * d : 256 * d + 256]
+    w2s[...] = f2_ref[...].astype(F32).T.astype(BF16)
+    for a in range(3):
+        w3s[:, 64 * a : 64 * a + 64] = f2_ref[288 * (2 - a) : 288 * (3 - a), :]
+    acc[464:512, :] = jnp.zeros((48, 128), F32)
     halo.wait()
-    compute(None, place.s, wide, w1_ref, w2_ref, w3_ref, sel_ref, cots, feat_ref, acc.at[0:432], acc.at[432:464],
+    compute(None, place.s, wide, w1s, w2s, w3s, sel_ref, cots, feats, acc.at[0:432], acc.at[432:464],
             px, maps, z1s, g2s, g1s)
+    feat_ref[...] = feats[...].T.astype(BF16)
     sent = all_reduce(place, acc, r0, s0, r1, r2, fin, sems)
-    sum_ref[...] = fin[...]
+    two_ref[0:432, :] = fin[0:432, 0:64]
+    two_ref[432:864, :] = fin[0:432, 64:128]
+    one = fin[432:464, :].T
+    for t in range(27):
+        one_ref[t] = one[4 * t : 4 * t + 4]
     halo.drain()
     for copy in sent:
         copy.wait_send()
 
 
 def local(crop, filter_one, filter_two, cotangent):
-    planes = crop[0].reshape(4, 4, 32, 2, 32, 2).transpose(1, 3, 5, 0, 2, 4).reshape(4, 16, LANES)
-    cot = cotangent.reshape(64, 256)
     sel = jnp.asarray(tap_selection(), BF16)
-    taps = jnp.pad(filter_one.reshape(108, 32), ((0, 20), (0, 0)))
-    w1 = jnp.einsum("to,tdk->dok", taps, sel.reshape(128, 8, 256), preferred_element_type=F32)
-    w1 = w1.astype(BF16).reshape(256, 256)
-    f2 = filter_two.reshape(864, 64)
-    w2 = f2.T
-    w3 = jnp.concatenate([f2[576:864], f2[288:576], f2[0:288]], axis=1)
     buffers, sems = reduce_scratch()
-    feat, sums = pl.pallas_call(
+    feat, one, two = pl.pallas_call(
         whole_kernel,
-        out_shape=(jax.ShapeDtypeStruct((64, 256), BF16), jax.ShapeDtypeStruct((512, 128), F32)),
+        out_shape=(
+            jax.ShapeDtypeStruct((256, 64), BF16),
+            jax.ShapeDtypeStruct((27, 4, 32), F32),
+            jax.ShapeDtypeStruct((864, 64), F32),
+        ),
         scratch_shapes=[
             pltpu.VMEM((14, 16, LANES), BF16),
             pltpu.VMEM((3, 64, 256), BF16),
@@ -390,6 +423,14 @@
             pltpu.VMEM((512, LANES), BF16),
             pltpu.VMEM((256, LANES), BF16),
             pltpu.VMEM((512, LANES), BF16),
+            pltpu.VMEM((1024, 64), F32),
+            pltpu.VMEM((128, 512), BF16),
+            pltpu.VMEM((64, LANES), BF16),
+            pltpu.VMEM((128, 32), F32),
+            pltpu.VMEM((256, 256), BF16),
+            pltpu.VMEM((64, 864), BF16),
+            pltpu.VMEM((288, 192), BF16),
+            pltpu.VMEM((64, 256), F32),
             *buffers,
             pltpu.SemaphoreType.DMA((6,)),
             pltpu.SemaphoreType.DMA((6,)),
@@ -398,10 +439,15 @@
         compiler_params=pltpu.CompilerParams(
             vmem_limit_bytes=60 * 1024 * 1024, collective_id=0, has_side_effects=True
         ),
-    )(planes, w1, w2, w3, sel, cot)
-    two = jnp.concatenate([sums[0:432, 0:64], sums[0:432, 64:128]]).reshape(3, 3, 3, 32, 64)
-    one = sums[432:464].T[0:108].reshape(3, 3, 3, 4, 32)
-    return feat.reshape(1, 64, 1, 16, 16), one, two
+    )(
+        crop.reshape(1024, 64),
+        filter_one.reshape(27, 4, 32),
+        filter_two.reshape(864, 64),
+        sel,
+        cotangent.transpose(0, 2, 3, 4, 1).reshape(256, 64),
+    )
+    feat = feat.reshape(1, 1, 16, 16, 64).transpose(0, 4, 1, 2, 3)
+    return feat, one.reshape(3, 3, 3, 4, 32), two.reshape(3, 3, 3, 32, 64)
 
 
 def solution(mesh):

time: 67.3 us -> 46.4 us (0.69)
  local copies, waits for them, and re-layouts: 22.3 us -> 3.92 us
  other arithmetic: 1.57 us -> 0 us
  matrix products: 0.87 us -> 0 us
    transpose x2 -> x0, local copies, waits for them, and re-layouts: 11.4 us -> none  [the longest x1 10.7 us: local(): crop[0].reshape(4, 4, 32, 2, 32, 2).transpose(1, 3, 5, 0, 2, 4)]
    reshape x6 -> x0, local copies, waits for them, and re-layouts: 3.42 us -> none  [the longest x1 1.19 us: local(): crop[0].reshape(4, 4, 32, 2, 32, 2).transpose(1, 3, 5, 0, 2, 4)]
    concatenate x2 -> x0, other arithmetic: 1.57 us -> none  [the longest x1 0.8 us: local(): jnp.concatenate([sums[0:432, 0:64], sums[0:432, 64:128]])]
    pallas_call x1 -> x0, local copies, waits for them, and re-layouts: 1.49 us -> none  [local(): pl.pallas_call(whole_kernel, out_shape=(jax.ShapeDtypeStruct((64, 256), B...]
    slice x3 -> x0, local copies, waits for them, and re-layouts: 1.28 us -> none  [the longest x1 1.15 us: local(): sums[0:432, 0:64]]
    dot_general x1 -> x0, matrix products: 0.87 us -> none  [local(): jnp.einsum('to,tdk->dok', taps, sel.reshape(128, 8, 256), preferred_eleme...]
    unnamed x9 -> x5, local copies, waits for them, and re-layouts: 4.68 us -> 3.92 us
where the time goes in v3:
time: 46.4 us; the launch traced here: 46.2 us
  Pallas kernels  41.6 us (90%)
  local copies, waits for them, and re-layouts  3.92 us (8%)
  between operations  0.65 us (1%)
    pallas_call x1, Pallas kernels, local(): pl.pallas_call(whole_kernel, out_shape=(jax.ShapeDtypeStruct((256, 64), B...  41.6 us
    unnamed x5, local copies, waits for them, and re-layouts  3.92 us

profile of v3, /device:TPU:1, one launch (start us, length us, event | category | flops | bytes accessed | tf_op | source)
XLA Modules:
  0.0 46.2 jit_solution(6258449445752395609)
XLA Ops:
  0.6 41.6 %shard_map.76 = (bf16[256,64]{1,0:T(8,128)(2,1)}, f32[27,4,32]{2,1,0:T(4,128)}, f32[864,64]{1,0:T(8,128)}) custom-call(bf16[1024,64]{1,0:T(8,128)(2,1)} %bitcast.12, bf16[27,4,32]{2,1,0:T(4,128)(2,1)} %bitcast.17, bf16[864,64]{1,0:T(8,128)(2,1)} %bitcast.13, bf16[128,2048]{1,0:T(8,128)(2,1)} %constant.2.clone.sel_ref, bf16[256,64]{1,0:T(8,128)(2,1)} %bitcast.14), custom_call_target="tpu_custom_call" | custom-call | tf_op jit(solution)/shard_map/pallas_call | solution.py:411
  42.3 0.0 copy-start
  42.3 1.5 %copy.11 = bf16[1,64,1,16,16]{1,4,3,2,0:T(8,128)(2,1)} copy(bf16[1,64,1,16,16]{1,4,3,2,0:T(8,128)(2,1)} %bitcast.15) | data formatting | bytes 65536
  43.8 0.0 copy-done
  43.8 0.6 %copy.12 = f32[3,3,3,4,32]{4,3,2,1,0:T(4,128)} copy(f32[3,3,3,4,32]{4,3,2,1,0:T(4,128)S(1)} %bitcast.16) | data formatting | bytes 27648
  44.4 1.8 %copy.13 = f32[3,3,3,32,64]{4,3,2,1,0:T(8,128)} copy(f32[3,3,3,32,64]{4,3,2,1,0:T(8,128)} %bitcast.11) | data formatting | bytes 442368
Async XLA Ops:
  42.3 1.5 %copy-start = (f32[27,4,32]{2,1,0:T(4,128)S(1)}, f32[27,4,32]{2,1,0:T(4,128)}, u32[]{:S(2)}) copy-start(f32[27,4,32]{2,1,0:T(4,128)} %get-tuple-element.7) | copy-start | bytes 41476

commit v4 on v1

v4 whole, which is shorter than its diff:
```python
import functools

import jax
import jax.numpy as jnp
import numpy as np
from jax import lax
from jax.experimental import pallas as pl
from jax.experimental.pallas import tpu as pltpu
from jax.sharding import PartitionSpec as P

F32, BF16 = jnp.float32, jnp.bfloat16
LANES = 1024


def leaky(value):
    return jnp.where(value > 0, value, 0.3 * value)


def dot_nn(a, b):
    return lax.dot_general(a, b, (((1,), (0,)), ((), ())), preferred_element_type=F32)


def dot_nt(a, b):
    return lax.dot_general(a, b, (((1,), (1,)), ((), ())), preferred_element_type=F32)


def split2(value):
    high = value.astype(BF16)
    return high, (value - high.astype(F32)).astype(BF16)


def tap_selection():
    table = np.zeros((128, 8, 256), np.float32)
    for d in range(8):
        dp, dq, dr = d // 4, d // 2 % 2, d % 2
        for pi in range(4):
            for sq in range(2):
                for sr in range(2):
                    for qe in range(2):
                        for re in range(2):
                            qi = (1 + qe) if sq == 0 else (0 if qe else 3)
                            ri = (1 + re) if sr == 0 else (0 if re else 3)
                            a, b, c = pi - dp, qi - dq, ri - dr
                            if min(a, b, c) < 0 or max(a, b, c) > 2:
                                continue
                            for i in range(4):
                                k = pi * 64 + (sq * 2 + sr) * 16 + (qe * 2 + re) * 4 + i
                                table[((a * 3 + b) * 3 + c) * 4 + i, d, k] = 1
    return table.reshape(128, 2048)


def lane_masks(rows):
    lane = lax.broadcasted_iota(jnp.int32, (rows, LANES), 1)
    return lane % 32, lane // 32


def ones(mask):
    return jnp.where(mask, 1.0, 0.0).astype(BF16)


def rolled(value, amount):
    return pltpu.roll(value, amount % LANES, 1)


NX, NY, NZH, NZL = 4, 4, 2, 4
ROWS = 16
HALF = NX * NY * ROWS
MESH = pl.DeviceIdType.MESH


class Place:
    def __init__(self):
        dp, self.s = lax.axis_index("dp"), lax.axis_index("space")
        self.zh, self.x = dp // NX, dp % NX
        self.core = self.s % 2
        self.y = self.s // 2 % NY
        self.zl = self.s // 2 // NY
        self.z = self.zh * NZL + self.zl

    def at(self, x, y, z, core):
        return {"dp": z // NZL * NX + x, "space": (z % NZL * NY + y) * 2 + core}

    def plane_peer(self, dx, dy):
        x, y = (self.x + dx) % NX, (self.y + dy) % NY
        return self.at(x, y, self.z, self.core), x * NY + y

    def plane_source(self, dx, dy):
        return (self.x - dx + NX) % NX * NY + (self.y - dy + NY) % NY

    def depth_peer(self, dz):
        return self.at(self.x, self.y, (self.z + dz) % (NZH * NZL), self.core)

    def depth_source(self, dz):
        return (self.z - dz + NZH * NZL) % (NZH * NZL)

    def partner(self):
        return self.at(self.x, self.y, self.z, 1 - self.core)


def plane_offsets():
    far = lambda d: min(d[0], NX - d[0]) + min(d[1], NY - d[1])
    every = [(dx, dy) for dx in range(NX) for dy in range(NY)]
    return sorted(every, key=lambda d: -far(d))[:-1]


def depth_offsets():
    count = NZH * NZL
    return sorted(range(1, count), key=lambda d: -min(d, count - d))


def remote(src, dst, send, recv, peer):
    copy = pltpu.make_async_remote_copy(
        src_ref=src, dst_ref=dst, send_sem=send, recv_sem=recv, device_id=peer, device_id_type=MESH
    )
    return copy


def started(src, dst, send, recv, peer):
    copy = remote(src, dst, send, recv, peer)
    copy.start()
    return copy


def rows16(start):
    return pl.ds(pl.multiple_of(start, ROWS), ROWS)


def greet(place):
    barrier = pltpu.get_barrier_semaphore()
    count = lax.axis_size("space")
    peers = [place.plane_peer(dx, dy)[0] for dx, dy in plane_offsets()]
    peers += [place.depth_peer(d) for d in depth_offsets()]
    peers += [{"space": (place.s + hop + count) % count} for hop in (1, -1, 2, -2)]
    peers += [place.partner()]
    for peer in peers:
        pl.semaphore_signal(barrier, inc=1, device_id=peer, device_id_type=MESH)
    return lambda: pl.semaphore_wait(barrier, len(peers))


HALO_MOVES = ((1, 3, 1, 4), (-1, 0, 1, 9), (1, 1, 2, 2), (-1, 1, 2, 10), (1, 0, 1, 1), (-1, 3, 1, 12), (2, 3, 1, 0), (-2, 0, 1, 13))


class Halo:
    def __init__(self, place, wide, cots, send, recv):
        self.s, self.count = place.s, lax.axis_size("space")
        self.items = {}
        for k, (hop, own, planes, to) in enumerate(HALO_MOVES):
            self.add(to, hop, wide.at[5 + own : 5 + own + planes], wide.at[to : to + planes], send.at[k], recv.at[k])
            if k == 3:
                self.add("left", 1, cots.at[1], cots.at[0], send.at[8], recv.at[8])
                self.add("right", -1, cots.at[1], cots.at[2], send.at[9], recv.at[9])

    def add(self, name, hop, src, dst, send, recv):
        peer = {"space": (self.s + hop + self.count) % self.count}
        self.items[name] = (hop, dst, remote(src, dst, send, recv, peer))

    def exists(self, hop):
        there = self.s + hop
        return (there >= 0) & (there < self.count)

    def start(self):
        for hop, dst, copy in self.items.values():
            pl.when(self.exists(hop))(copy.start)

    def clear(self):
        for hop, dst, copy in self.items.values():

            @pl.when(jnp.logical_not(self.exists(-hop)))
            def _(dst=dst):
                dst[...] = jnp.zeros(dst.shape, BF16)

    def wait(self, *names):
        for name in names:
            hop, dst, copy = self.items[name]
            pl.when(self.exists(-hop))(copy.wait_recv)

    def drain(self):
        for hop, dst, copy in self.items.values():
            pl.when(self.exists(hop))(copy.wait_send)


class LargeFlow:
    def __init__(self, place, acc, r0, s0, r1, r2, fin, sems):
        self.place, self.acc, self.r0, self.s0, self.r1, self.r2, self.fin = place, acc, r0, s0, r1, r2, fin
        self.sems, self.sent = sems, []
        self.peers = [place.plane_peer(dx, dy) for dx, dy in plane_offsets()]
        self.own = place.x * NY + place.y
        self.mine = place.core * HALF
        self.other = HALF - self.mine
        self.order = [j for _, j in self.peers] + [self.own]

    def go(self, *args):
        copy = started(*args)
        self.sent.append(copy)
        return copy

    def halves(self):
        send, recv = self.sems[0:2]
        self.step0 = [
            self.go(self.acc.at[rows16(self.other + j * ROWS)], self.r0.at[rows16(j * ROWS)], send.at[k], recv.at[k],
                    self.place.partner())
            for k, j in enumerate(self.order)
        ]

    def shares(self):
        send, recv = self.sems[2:4]
        self.step1 = []

        def pass_on(k):
            peer, j = self.peers[k]
            self.step1.append(self.go(self.s0.at[rows16(j * ROWS)], self.r1.at[k], send.at[k], recv.at[k], peer))

        count = len(self.peers)
        for k, j in enumerate(self.order):
            self.step0[k].wait_recv()
            total = self.acc[rows16(self.mine + j * ROWS), :] + self.r0[rows16(j * ROWS), :]
            if k < count:
                self.s0[rows16(j * ROWS), :] = total.astype(BF16)
            else:
                self.r2[self.place.z] = total
            if k >= 1:
                pass_on(k - 1)

    def depth(self):
        total = self.r2[self.place.z]
        for k in range(len(self.peers) - 1, -1, -1):
            self.step1[k].wait_recv()
            total = total + self.r1[k].astype(F32)
        self.r2[self.place.z] = total
        send, recv = self.sems[4:6]
        here = self.r2.at[self.place.z]
        self.step2 = [
            self.go(here, here, send.at[k], recv.at[k], self.place.depth_peer(d)) for k, d in enumerate(depth_offsets())
        ]

    def gather(self):
        for copy in self.step2:
            copy.wait_recv()
        total = self.r2[0]
        for z in range(1, NZH * NZL):
            total = total + self.r2[z]
        at = rows16(self.mine + self.own * ROWS)
        self.fin[at, :] = total.astype(BF16)
        send, recv = self.sems[6:8]
        here = self.fin.at[at]
        self.step3 = [self.go(here, here, send.at[k], recv.at[k], peer) for k, (peer, _) in enumerate(self.peers)]
        self.step4 = []
        self.hand_over(self.own)

    def hand_over(self, share):
        send, recv = self.sems[8:10]
        k = len(self.step4)
        here = self.fin.at[rows16(self.mine + share * ROWS)]
        self.step4.append(self.go(here, here, send.at[k], recv.at[k], self.place.partner()))

    def give_back(self):
        offsets = plane_offsets()
        for k in range(len(offsets) - 1, -1, -1):
            self.step3[k].wait_recv()
            self.hand_over(self.place.plane_source(*offsets[k]))

    def finish(self):
        for copy in self.step4:
            copy.wait_recv()


class SmallFlow:
    def __init__(self, place, acc, r0, q1, q2, out, sems):
        self.place, self.acc, self.r0, self.q1, self.q2, self.out = place, acc, r0, q1, q2, out
        self.sems, self.sent = sems, []
        self.mine = place.core * ROWS
        self.own = place.x * NY + place.y

    def go(self, *args):
        copy = started(*args)
        self.sent.append(copy)
        return copy

    def halves(self):
        send, recv = self.sems[0:2]
        self.step0 = self.go(self.acc.at[rows16(ROWS - self.mine)], self.r0, send.at[0], recv.at[0], self.place.partner())

    def plane(self):
        self.step0.wait_recv()
        self.q1[self.own] = (self.acc[rows16(self.mine), :] + self.r0[...]).astype(BF16)
        send, recv = self.sems[2:4]
        here = self.q1.at[self.own]
        self.step1 = [
            self.go(here, here, send.at[k], recv.at[k], self.place.plane_peer(dx, dy)[0])
            for k, (dx, dy) in enumerate(plane_offsets())
        ]

    def depth(self):
        for copy in self.step1:
            copy.wait_recv()
        total = self.q1[0].astype(F32)
        for j in range(1, NX * NY):
            total = total + self.q1[j].astype(F32)
        self.q2[self.place.z] = total
        send, recv = self.sems[4:6]
        here = self.q2.at[self.place.z]
        self.step2 = [
            self.go(here, here, send.at[k], recv.at[k], self.place.depth_peer(d)) for k, d in enumerate(depth_offsets())
        ]

    def give_back(self):
        for copy in self.step2:
            copy.wait_recv()
        total = self.q2[0]
        for z in range(1, NZH * NZL):
            total = total + self.q2[z]
        at = rows16(self.mine)
        self.out[at, :] = total
        send, recv = self.sems[6:8]
        here = self.out.at[at]
        self.step3 = self.go(here, here, send.at[0], recv.at[0], self.place.partner())

    def finish(self):
        self.step3.wait_recv()


def flow_scratch():
    n, depth = NX * NY, NZH * NZL
    dma = pltpu.SemaphoreType.DMA
    large = [
        pltpu.VMEM((2 * HALF, 128), F32),
        pltpu.VMEM((HALF, 128), F32),
        pltpu.VMEM((HALF, 128), BF16),
        pltpu.VMEM((n - 1, ROWS, 128), BF16),
        pltpu.VMEM((depth, ROWS, 128), F32),
        pltpu.VMEM((2 * HALF, 128), BF16),
    ]
    large_sems = [dma((k,)) for k in (n, n, n - 1, n - 1, depth - 1, depth - 1, n - 1, n - 1, n, n)]
    small = [
        pltpu.VMEM((2 * ROWS, 128), F32),
        pltpu.VMEM((ROWS, 128), F32),
        pltpu.VMEM((n, ROWS, 128), BF16),
        pltpu.VMEM((depth, ROWS, 128), F32),
        pltpu.VMEM((2 * ROWS, 128), F32),
    ]
    small_sems = [dma((k,)) for k in (1, 1, n - 1, n - 1, depth - 1, depth - 1, 1, 1)]
    return large, large_sems, small, small_sems


def iota2(shape):
    return lax.broadcasted_iota(jnp.int32, shape, 0), lax.broadcasted_iota(jnp.int32, shape, 1)


def flatten_planes(crop_ref, wide, cf, lp, fs):
    cf[...] = crop_ref[...].astype(F32)
    for h in range(32):
        pair = [cf[pl.ds(2 * h + e, 16, stride=64), :] for e in range(2)]
        lp[h // 4 * 16 : h // 4 * 16 + 16, h % 4 * 128 : h % 4 * 128 + 128] = jnp.concatenate(pair, axis=1).astype(BF16)
    k, n = iota2((512, 512))
    to = (k // 64 % 2 * 2 + k % 2) * 128 + k // 128 * 32 + k % 64 // 2
    moved = dot_nn(lp[...], ones(to == n))
    for block in range(8):
        for c in range(4):
            fs[16 * c : 16 * c + 16, 128 * block : 128 * block + 128] = moved[
                16 * block : 16 * block + 16, 128 * c : 128 * c + 128
            ].astype(BF16)
    m, n = iota2((64, 64))
    rows = dot_nn(ones(m // 4 % 4 * 16 + m % 4 * 4 + m // 16 == n), fs[...])
    for p in range(4):
        wide[5 + p] = rows[16 * p : 16 * p + 16].astype(BF16)


class Local:
    def __init__(self, s, wide, cots, px, maps, z1s, g2s, g1s, w1s, w2s, w3s):
        self.wide, self.cots, self.px, self.maps = wide, cots, px, maps
        self.z1s, self.g2s, self.g1s, self.w1s, self.w2s, self.w3s = z1s, g2s, g1s, w1s, w2s, w3s
        r, q = lane_masks(16)
        row = lax.broadcasted_iota(jnp.int32, (16, LANES), 0)
        q_odd, r_odd = row // 8 == 1, row // 4 % 2 == 1
        self.r_up, self.r_down = ones(r_odd & (r != 0)), ones(~r_odd & (r != 31))
        self.q_up, self.q_down = ones(q_odd & (q != 0)), ones(~q_odd & (q != 31))
        self.left_ok = jnp.where(s > 0, 0.125, 0.0)
        self.right_ok = jnp.where(s < lax.axis_size("space") - 1, 0.125, 0.0)
        r, q = lane_masks(32)
        self.keep, self.keep_ones = {}, {}
        for db in (-1, 0, 1):
            for dc in (-1, 0, 1):
                ok = jnp.ones((32, LANES), jnp.bool_)
                if db:
                    ok = ok & ((q != 0) if db < 0 else (q != 31))
                if dc:
                    ok = ok & ((r != 0) if dc < 0 else (r != 31))
                self.keep[db, dc] = ok
                self.keep_ones[db, dc] = ones(ok)
        k, n = iota2((128, 512))
        self.spread = ones((n // 64 == k // 16) & (n % 32 // 2 == k % 16))
        k, n = iota2((256, 64))
        self.collect = ones((k // 64 == n // 16) & (k % 32 // 2 == n % 16))

    def patch(self, *planes):
        for plane in planes:
            x = self.wide[plane]
            xr = rolled(x, 1) * self.r_up + rolled(x, -1) * self.r_down
            xq = rolled(x, 32) * self.q_up + rolled(x, -32) * self.q_down
            xqr = rolled(xr, 32) * self.q_up + rolled(xr, -32) * self.q_down
            for k, piece in enumerate((x, xr, xq, xqr)):
                self.px[plane * 64 + k * 16 : plane * 64 + k * 16 + 16, :] = piece

    def first(self, plane):
        z = dot_nn(self.w1s[...], self.px[plane * 128 : plane * 128 + 256, :])
        if plane in (2, 3):
            self.z1s[(plane - 2) * 256 : (plane - 1) * 256, :] = z.astype(BF16)
        z = leaky(z)
        total = z[0:32]
        for d in range(1, 8):
            total = total + z[d * 32 : d * 32 + 32]
        a1 = (total * (self.left_ok if plane < 2 else self.right_ok if plane > 3 else 0.125)).astype(BF16)
        for b in range(3):
            for c in range(3):
                v = a1
                if (b, c) != (1, 1):
                    v = rolled(v, -(32 * (b - 1) + (c - 1))) * self.keep_ones[b - 1, c - 1]
                at = plane * 288 + (b * 3 + c) * 32
                self.maps[at : at + 32, :] = v

    def second(self, plane):
        z = dot_nn(self.w2s[...], self.maps[plane * 288 : plane * 288 + 864, :])
        cot = self.cots[(0, 1, 1, 2)[plane]]
        wide = jnp.concatenate([dot_nn(cot[:, 0:128], self.spread), dot_nn(cot[:, 128:256], self.spread)], axis=1) * 0.125
        self.g2s[plane * 64 : plane * 64 + 64, :] = jnp.where(z > 0, wide, 0.3 * wide).astype(BF16)
        return leaky(z)

    def features(self, pair, feats):
        high, low = split2(pair)
        for j in range(4):
            lanes = slice(256 * j, 256 * j + 256)
            feats[:, 64 * j : 64 * j + 64] = (
                dot_nn(high[:, lanes], self.collect) + dot_nn(low[:, lanes], self.collect)
            ) * 0.125

    def grad_two(self, acc, start):
        at = pl.ds(pl.multiple_of(start, HALF), HALF)
        parts = []
        for fold in range(2):
            part = None
            for p in range(2):
                first = pl.multiple_of(start + 288 * (p + 1) + 432 * fold, 16)
                term = dot_nt(self.maps[pl.ds(first, HALF), :], self.g2s[64 * (p + 1) : 64 * (p + 2), :])
                part = term if part is None else part + term
            parts.append(part)
        acc[at, :] = jnp.concatenate(parts, axis=1)

    def back(self, plane):
        u = dot_nn(self.w3s[...], self.g2s[plane * 64 : plane * 64 + 192, :])
        back = None
        for b in range(3):
            for c in range(3):
                v = u[(b * 3 + c) * 32 : (b * 3 + c) * 32 + 32]
                if (b, c) != (1, 1):
                    v = rolled(v, -(32 * (1 - b) + (1 - c)))
                    v = jnp.where(self.keep[1 - b, 1 - c], v, 0.0)
                back = v if back is None else back + v
        back = back * 0.125
        low = 0.3 * back
        for d in range(8):
            at = plane * 256 + d * 32
            self.g1s[at : at + 32, :] = jnp.where(self.z1s[at : at + 32, :].astype(F32) > 0, back, low).astype(BF16)

    def grad_one(self, sel_ref, acc):
        gram = dot_nt(self.g1s[0:256, :], self.px[256:512, :]) + dot_nt(self.g1s[256:512, :], self.px[384:640, :])
        total = None
        for d in range(8):
            high, low = split2(gram[d * 32 : d * 32 + 32])
            sel = sel_ref[:, d * 256 : d * 256 + 256]
            term = dot_nt(high, sel) + dot_nt(low, sel)
            total = term if total is None else total + term
        acc[...] = total


def whole_kernel(crop_hbm, f1_hbm, f2_hbm, sel_hbm, cot_hbm, feat_ref, one_ref, two_ref,
                 crop_ref, f1_ref, f2_ref, sel_ref, cot_ref, wide, cots, px, maps, z1s, g2s, g1s,
                 cf, lp, fs, f1s, w1s, w2s, w3s, feats, fetch, halo_send, halo_recv, *flows):
    place = Place()
    ready = greet(place)
    pairs = ((crop_hbm, crop_ref), (cot_hbm, cot_ref), (f1_hbm, f1_ref), (sel_hbm, sel_ref), (f2_hbm, f2_ref))
    fetched = [pltpu.make_async_copy(src, dst, fetch.at[k]) for k, (src, dst) in enumerate(pairs)]
    for copy in fetched:
        copy.start()
    halo = Halo(place, wide, cots, halo_send, halo_recv)
    halo.clear()
    local = Local(place.s, wide, cots, px, maps, z1s, g2s, g1s, w1s, w2s, w3s)
    large = LargeFlow(place, *flows[0:6], flows[6:16])
    small = SmallFlow(place, *flows[16:21], flows[21:29])
    fetched[0].wait()
    flatten_planes(crop_ref, wide, cf, lp, fs)
    fetched[1].wait()
    cots[1] = cot_ref[...].astype(F32).T.astype(BF16)
    ready()
    halo.start()
    fetched[2].wait()
    f1s[108:128, :] = jnp.zeros((20, 32), F32)
    for t in range(27):
        f1s[4 * t : 4 * t + 4, :] = f1_ref[t].astype(F32)
    fetched[3].wait()
    w1 = dot_nn(f1s[...].T.astype(BF16), sel_ref[...]).astype(BF16)
    for d in range(8):
        w1s[32 * d : 32 * d + 32, :] = w1[:, 256 * d : 256 * d + 256]
    fetched[4].wait()
    w2s[...] = f2_ref[...].astype(F32).T.astype(BF16)
    for a in range(3):
        w3s[:, 64 * a : 64 * a + 64] = f2_ref[288 * (2 - a) : 288 * (3 - a), :]
    local.patch(5, 6, 7, 8)
    halo.wait(4)
    local.patch(4)
    local.first(2)
    halo.wait(9)
    local.patch(9)
    local.first(3)
    halo.wait(2)
    local.patch(2, 3)
    local.first(1)
    halo.wait(10)
    local.patch(10, 11)
    local.first(4)
    pair = local.second(1)
    pair = pair + local.second(2)
    local.features(pair, feats)
    local.grad_two(large.acc, large.other)
    large.halves()
    local.grad_two(large.acc, large.mine)
    halo.wait(0, 1)
    local.patch(0, 1)
    local.first(0)
    halo.wait("left")
    local.second(0)
    halo.wait(12, 13)
    local.patch(12, 13)
    local.first(5)
    halo.wait("right")
    local.second(3)
    large.shares()
    local.back(0)
    local.back(1)
    local.grad_one(sel_ref, small.acc)
    small.halves()
    feat_ref[...] = feats[...].T.astype(BF16)
    small.plane()
    large.depth()
    large.gather()
    small.depth()
    large.give_back()
    small.give_back()
    large.finish()
    two_ref[0:432, :] = large.fin[0:432, 0:64].astype(F32)
    two_ref[432:864, :] = large.fin[0:432, 64:128].astype(F32)
    small.finish()
    one = small.out[...].T
    for t in range(27):
        one_ref[t] = one[4 * t : 4 * t + 4]
    halo.drain()
    for copy in large.sent + small.sent:
        copy.wait_send()


def local(crop, filter_one, filter_two, cotangent):
    sel = jnp.asarray(tap_selection(), BF16)
    large, large_sems, small, small_sems = flow_scratch()
    hbm = pl.BlockSpec(memory_space=pltpu.HBM)
    operands = (
        crop.reshape(1024, 64),
        filter_one.reshape(27, 4, 32),
        filter_two.reshape(864, 64),
        sel,
        cotangent.transpose(0, 2, 3, 4, 1).reshape(256, 64),
    )
    feat, one, two = pl.pallas_call(
        whole_kernel,
        out_shape=(
            jax.ShapeDtypeStruct((256, 64), BF16),
            jax.ShapeDtypeStruct((27, 4, 32), F32),
            jax.ShapeDtypeStruct((864, 64), F32),
        ),
        in_specs=[hbm] * 5,
        scratch_shapes=[
            pltpu.VMEM((1024, 64), BF16),
            pltpu.VMEM((27, 4, 32), BF16),
            pltpu.VMEM((864, 64), BF16),
            pltpu.VMEM((128, 2048), BF16),
            pltpu.VMEM((256, 64), BF16),
            pltpu.VMEM((14, 16, LANES), BF16),
            pltpu.VMEM((3, 64, 256), BF16),
            pltpu.VMEM((896, LANES), BF16),
            pltpu.VMEM((1728, LANES), BF16),
            pltpu.VMEM((512, LANES), BF16),
            pltpu.VMEM((256, LANES), BF16),
            pltpu.VMEM((512, LANES), BF16),
            pltpu.VMEM((1024, 64), F32),
            pltpu.VMEM((128, 512), BF16),
            pltpu.VMEM((64, LANES), BF16),
            pltpu.VMEM((128, 32), F32),
            pltpu.VMEM((256, 256), BF16),
            pltpu.VMEM((64, 864), BF16),
            pltpu.VMEM((288, 192), BF16),
            pltpu.VMEM((64, 256), F32),
            pltpu.SemaphoreType.DMA((5,)),
            pltpu.SemaphoreType.DMA((10,)),
            pltpu.SemaphoreType.DMA((10,)),
            *large,
            *large_sems,
            *small,
            *small_sems,
        ],
        compiler_params=pltpu.CompilerParams(
            vmem_limit_bytes=32 * 1024 * 1024, collective_id=0, has_side_effects=True
        ),
    )(*[pltpu.with_memory_space_constraint(value, pltpu.HBM) for value in operands])
    feat = feat.reshape(1, 1, 16, 16, 64).transpose(0, 4, 1, 2, 3)
    return feat, one.reshape(3, 3, 3, 4, 32), two.reshape(3, 3, 3, 32, 64)


def solution(mesh):
    placed = (P("dp", None, "space", None, None), P(), P(), P("dp", None, "space", None, None))
    return jax.shard_map(
        local, mesh=mesh, in_specs=placed, out_specs=(P("dp", None, "space", None, None), P(), P()), check_vma=False
    )
```

time: 350 us -> 39.9 us (0.11)
  waiting for transfers between devices: 174 us -> 0 us
  blocking collectives: 81.4 us -> 0 us
  local copies, waits for them, and re-layouts: 53 us -> 2.02 us
  Pallas kernels: 7.39 us -> 37.1 us
  starting transfers between devices: 16.6 us -> 0 us
  between operations: 14.3 us -> 0.64 us
    psum x1 -> x0, waiting for transfers between devices: 170 us -> none  [local(): two, one = lax.psum((two, one), ('dp', 'space'))]
    psum x1 -> x0, blocking collectives: 81.4 us -> none  [local(): two, one = lax.psum((two, one), ('dp', 'space'))]
    slice x8 -> x0, local copies, waits for them, and re-layouts: 33.1 us -> none  [the longest x3 21.3 us: local(): planes[0:1]]
    pallas_call x1, Pallas kernels: 7.39 us -> 37.1 us  [local(): pl.pallas_call(whole_kernel, out_shape=(jax.ShapeDtypeStruct((256, 64), B...]
    ppermute x6 -> x0, starting transfers between devices: 16.6 us -> none  [shift_planes(): lax.ppermute(value, axis, [(j, j + hops) for j in range(count) if 0 <= j...]
    transpose x1 -> x0, local copies, waits for them, and re-layouts: 10.7 us -> none  [local(): crop[0].reshape(4, 4, 32, 2, 32, 2).transpose(1, 3, 5, 0, 2, 4)]
  transfers between devices with their start and end apart: 7 -> 0, of which waited for: 2 -> 0; matrix products, arithmetic and copies ran while one was open for 11% -> 0% of each run, Pallas kernels for 0% -> 0%
where the time goes in v4:
time: 39.9 us; the launch traced here: 39.8 us
  Pallas kernels  37.1 us (93%)
  local copies, waits for them, and re-layouts  2.02 us (5%)
  between operations  0.64 us (2%)
    pallas_call x1, Pallas kernels, local(): pl.pallas_call(whole_kernel, out_shape=(jax.ShapeDtypeStruct((256, 64), B...  37.1 us
    unnamed x3, local copies, waits for them, and re-layouts  2.02 us

profile of v4, /device:TPU:1, one launch (start us, length us, event | category | flops | bytes accessed | tf_op | source)
XLA Modules:
  0.0 39.8 jit_solution(1457577310282531774)
XLA Ops:
  0.6 37.1 %shard_map.76 = (bf16[256,64]{1,0:T(8,128)(2,1)S(1)}, f32[27,4,32]{2,1,0:T(4,128)S(1)}, f32[864,64]{1,0:T(8,128)S(1)}) custom-call(bf16[1024,64]{1,0:T(8,128)(2,1)} %bitcast.14, bf16[27,4,32]{2,1,0:T(4,128)(2,1)} %bitcast.17, bf16[864,64]{1,0:T(8,128)(2,1)} %bitcast.15, bf16[128,2048]{1,0:T(8,128)(2,1)} %constant.2.clone.sel_hbm, bf16[256,64]{1,0:T(8,128)(2,1)} %bitcast.16), custom_call_target="tpu_custom_call" | custom-call | tf_op jit(solution)/shard_map/pallas_call | solution.py:571
  37.8 0.6 %copy.11 = bf16[1,64,1,16,16]{1,4,3,2,0:T(8,128)(2,1)} copy(bf16[1,64,1,16,16]{1,4,3,2,0:T(8,128)(2,1)S(1)} %bitcast.12) | data formatting | bytes 65536
  38.4 0.6 %copy.12 = f32[3,3,3,4,32]{4,3,2,1,0:T(4,128)} copy(f32[3,3,3,4,32]{4,3,2,1,0:T(4,128)S(1)} %bitcast.13) | data formatting | bytes 27648
  39.0 0.8 %copy.13 = f32[3,3,3,32,64]{4,3,2,1,0:T(8,128)} copy(f32[3,3,3,32,64]{4,3,2,1,0:T(8,128)S(1)} %bitcast.11) | data formatting | bytes 442368

commit v5 on v4

--- a/solution.py
+++ b/solution.py
@@ -80,26 +80,24 @@
     def at(self, x, y, z, core):
         return {"dp": z // NZL * NX + x, "space": (z % NZL * NY + y) * 2 + core}
 
-    def plane_peer(self, dx, dy):
-        x, y = (self.x + dx) % NX, (self.y + dy) % NY
-        return self.at(x, y, self.z, self.core), x * NY + y
-
-    def plane_source(self, dx, dy):
-        return (self.x - dx + NX) % NX * NY + (self.y - dy + NY) % NY
+    def plane_peers(self):
+        peers = []
+        for dx, dy, flip in plane_offsets():
+            x, y = (self.x + dx) % NX, (self.y + dy) % NY
+            core = 1 - self.core if flip else self.core
+            peers.append((self.at(x, y, self.z, core), core, core * HALF + (x * NY + y) * ROWS))
+        return peers
 
     def depth_peer(self, dz):
         return self.at(self.x, self.y, (self.z + dz) % (NZH * NZL), self.core)
 
-    def depth_source(self, dz):
-        return (self.z - dz + NZH * NZL) % (NZH * NZL)
-
     def partner(self):
         return self.at(self.x, self.y, self.z, 1 - self.core)
 
 
 def plane_offsets():
     far = lambda d: min(d[0], NX - d[0]) + min(d[1], NY - d[1])
-    every = [(dx, dy) for dx in range(NX) for dy in range(NY)]
+    every = [(dx, dy, flip) for dx in range(NX) for dy in range(NY) for flip in (1, 0)]
     return sorted(every, key=lambda d: -far(d))[:-1]
 
 
@@ -115,12 +113,6 @@
     return copy
 
 
-def started(src, dst, send, recv, peer):
-    copy = remote(src, dst, send, recv, peer)
-    copy.start()
-    return copy
-
-
 def rows16(start):
     return pl.ds(pl.multiple_of(start, ROWS), ROWS)
 
@@ -128,10 +120,9 @@
 def greet(place):
     barrier = pltpu.get_barrier_semaphore()
     count = lax.axis_size("space")
-    peers = [place.plane_peer(dx, dy)[0] for dx, dy in plane_offsets()]
+    peers = [peer for peer, _, _ in place.plane_peers()]
     peers += [place.depth_peer(d) for d in depth_offsets()]
     peers += [{"space": (place.s + hop + count) % count} for hop in (1, -1, 2, -2)]
-    peers += [place.partner()]
     for peer in peers:
         pl.semaphore_signal(barrier, inc=1, device_id=peer, device_id_type=MESH)
     return lambda: pl.semaphore_wait(barrier, len(peers))
@@ -179,167 +170,114 @@
             pl.when(self.exists(hop))(copy.wait_send)
 
 
-class LargeFlow:
-    def __init__(self, place, acc, r0, s0, r1, r2, fin, sems):
-        self.place, self.acc, self.r0, self.s0, self.r1, self.r2, self.fin = place, acc, r0, s0, r1, r2, fin
-        self.sems, self.sent = sems, []
-        self.peers = [place.plane_peer(dx, dy) for dx, dy in plane_offsets()]
-        self.own = place.x * NY + place.y
-        self.mine = place.core * HALF
-        self.other = HALF - self.mine
-        self.order = [j for _, j in self.peers] + [self.own]
-
-    def go(self, *args):
-        copy = started(*args)
-        self.sent.append(copy)
-        return copy
-
-    def halves(self):
-        send, recv = self.sems[0:2]
-        self.step0 = [
-            self.go(self.acc.at[rows16(self.other + j * ROWS)], self.r0.at[rows16(j * ROWS)], send.at[k], recv.at[k],
-                    self.place.partner())
-            for k, j in enumerate(self.order)
-        ]
-
-    def shares(self):
-        send, recv = self.sems[2:4]
-        self.step1 = []
-
-        def pass_on(k):
-            peer, j = self.peers[k]
-            self.step1.append(self.go(self.s0.at[rows16(j * ROWS)], self.r1.at[k], send.at[k], recv.at[k], peer))
-
-        count = len(self.peers)
-        for k, j in enumerate(self.order):
-            self.step0[k].wait_recv()
-            total = self.acc[rows16(self.mine + j * ROWS), :] + self.r0[rows16(j * ROWS), :]
-            if k < count:
-                self.s0[rows16(j * ROWS), :] = total.astype(BF16)
-            else:
-                self.r2[self.place.z] = total
-            if k >= 1:
-                pass_on(k - 1)
+class Flow:
+    def __init__(self, place, sems):
+        self.place, self.sems, self.sent = place, sems, []
+
+    def send(self, phase, items):
+        for src, dst, peer in items:
+            remote(src, dst, self.sems.at[0, phase], self.sems.at[1, phase], peer).start()
+
+    def arrive(self, phase, whole):
+        self.sent.append((phase, whole))
+        remote(whole, whole, self.sems.at[0, phase], self.sems.at[1, phase], self.place.partner()).wait_recv()
+
+    def drain(self):
+        for phase, whole in self.sent:
+            remote(whole, whole, self.sems.at[0, phase], self.sems.at[1, phase], self.place.partner()).wait_send()
+
+
+class LargeFlow(Flow):
+    def __init__(self, place, acc, accb, r1, r2, fin, sems):
+        super().__init__(place, sems)
+        self.acc, self.accb, self.r1, self.r2, self.fin = acc, accb, r1, r2, fin
+        self.peers = place.plane_peers()
+        self.own = place.core * HALF + (place.x * NY + place.y) * ROWS
+
+    def shares(self, half):
+        at = slice(half * HALF, half * HALF + HALF)
+        self.accb[at, :] = self.acc[at, :].astype(BF16)
+        for k, (peer, core, row) in enumerate(self.peers):
+            go = remote(self.accb.at[rows16(row)], self.r1.at[k], self.sems.at[0, 0], self.sems.at[1, 0], peer)
+            pl.when(core == half)(go.start)
 
     def depth(self):
-        total = self.r2[self.place.z]
-        for k in range(len(self.peers) - 1, -1, -1):
-            self.step1[k].wait_recv()
+        self.arrive(0, self.r1)
+        total = self.acc[rows16(self.own), :]
+        for k in range(len(self.peers)):
             total = total + self.r1[k].astype(F32)
         self.r2[self.place.z] = total
-        send, recv = self.sems[4:6]
         here = self.r2.at[self.place.z]
-        self.step2 = [
-            self.go(here, here, send.at[k], recv.at[k], self.place.depth_peer(d)) for k, d in enumerate(depth_offsets())
-        ]
+        self.send(1, [(here, here, self.place.depth_peer(d)) for d in depth_offsets()])
 
     def gather(self):
-        for copy in self.step2:
-            copy.wait_recv()
+        self.arrive(1, self.r2.at[1:])
         total = self.r2[0]
         for z in range(1, NZH * NZL):
             total = total + self.r2[z]
-        at = rows16(self.mine + self.own * ROWS)
-        self.fin[at, :] = total.astype(BF16)
-        send, recv = self.sems[6:8]
-        here = self.fin.at[at]
-        self.step3 = [self.go(here, here, send.at[k], recv.at[k], peer) for k, (peer, _) in enumerate(self.peers)]
-        self.step4 = []
-        self.hand_over(self.own)
-
-    def hand_over(self, share):
-        send, recv = self.sems[8:10]
-        k = len(self.step4)
-        here = self.fin.at[rows16(self.mine + share * ROWS)]
-        self.step4.append(self.go(here, here, send.at[k], recv.at[k], self.place.partner()))
-
-    def give_back(self):
-        offsets = plane_offsets()
-        for k in range(len(offsets) - 1, -1, -1):
-            self.step3[k].wait_recv()
-            self.hand_over(self.place.plane_source(*offsets[k]))
+        self.fin[rows16(self.own), :] = total.astype(BF16)
+        here = self.fin.at[rows16(self.own)]
+        self.send(2, [(here, here, peer) for peer, _, _ in self.peers])
 
     def finish(self):
-        for copy in self.step4:
-            copy.wait_recv()
-
-
-class SmallFlow:
-    def __init__(self, place, acc, r0, q1, q2, out, sems):
-        self.place, self.acc, self.r0, self.q1, self.q2, self.out = place, acc, r0, q1, q2, out
-        self.sems, self.sent = sems, []
+        self.arrive(2, self.fin.at[ROWS:])
+
+
+class SmallFlow(Flow):
+    def __init__(self, place, acc, accb, q1, q2, out, sems):
+        super().__init__(place, sems)
+        self.acc, self.accb, self.q1, self.q2, self.out = acc, accb, q1, q2, out
         self.mine = place.core * ROWS
-        self.own = place.x * NY + place.y
-
-    def go(self, *args):
-        copy = started(*args)
-        self.sent.append(copy)
-        return copy
-
-    def halves(self):
-        send, recv = self.sems[0:2]
-        self.step0 = self.go(self.acc.at[rows16(ROWS - self.mine)], self.r0, send.at[0], recv.at[0], self.place.partner())
-
-    def plane(self):
-        self.step0.wait_recv()
-        self.q1[self.own] = (self.acc[rows16(self.mine), :] + self.r0[...]).astype(BF16)
-        send, recv = self.sems[2:4]
-        here = self.q1.at[self.own]
-        self.step1 = [
-            self.go(here, here, send.at[k], recv.at[k], self.place.plane_peer(dx, dy)[0])
-            for k, (dx, dy) in enumerate(plane_offsets())
-        ]
+        self.own = place.core * NX * NY + place.x * NY + place.y
+
+    def shares(self):
+        for half in range(2):
+            self.accb[half] = self.acc[half * ROWS : half * ROWS + ROWS, :].astype(BF16)
+        self.q1[self.own] = self.accb[self.place.core]
+        there = self.q1.at[self.own]
+        self.send(0, [(self.accb.at[core], there, peer) for peer, core, _ in self.place.plane_peers()])
 
     def depth(self):
-        for copy in self.step1:
-            copy.wait_recv()
+        self.arrive(0, self.q1.at[1:])
         total = self.q1[0].astype(F32)
-        for j in range(1, NX * NY):
+        for j in range(1, 2 * NX * NY):
             total = total + self.q1[j].astype(F32)
         self.q2[self.place.z] = total
-        send, recv = self.sems[4:6]
         here = self.q2.at[self.place.z]
-        self.step2 = [
-            self.go(here, here, send.at[k], recv.at[k], self.place.depth_peer(d)) for k, d in enumerate(depth_offsets())
-        ]
+        self.send(1, [(here, here, self.place.depth_peer(d)) for d in depth_offsets()])
 
     def give_back(self):
-        for copy in self.step2:
-            copy.wait_recv()
+        self.arrive(1, self.q2.at[1:])
         total = self.q2[0]
         for z in range(1, NZH * NZL):
             total = total + self.q2[z]
-        at = rows16(self.mine)
-        self.out[at, :] = total
-        send, recv = self.sems[6:8]
-        here = self.out.at[at]
-        self.step3 = self.go(here, here, send.at[0], recv.at[0], self.place.partner())
+        self.out[rows16(self.mine), :] = total
+        here = self.out.at[rows16(self.mine)]
+        self.send(2, [(here, here, self.place.partner())])
 
     def finish(self):
-        self.step3.wait_recv()
+        self.arrive(2, self.out.at[0:ROWS])
 
 
 def flow_scratch():
-    n, depth = NX * NY, NZH * NZL
-    dma = pltpu.SemaphoreType.DMA
+    n, depth = 2 * NX * NY, NZH * NZL
     large = [
         pltpu.VMEM((2 * HALF, 128), F32),
-        pltpu.VMEM((HALF, 128), F32),
-        pltpu.VMEM((HALF, 128), BF16),
+        pltpu.VMEM((2 * HALF, 128), BF16),
         pltpu.VMEM((n - 1, ROWS, 128), BF16),
         pltpu.VMEM((depth, ROWS, 128), F32),
         pltpu.VMEM((2 * HALF, 128), BF16),
+        pltpu.SemaphoreType.DMA((2, 3)),
     ]
-    large_sems = [dma((k,)) for k in (n, n, n - 1, n - 1, depth - 1, depth - 1, n - 1, n - 1, n, n)]
     small = [
         pltpu.VMEM((2 * ROWS, 128), F32),
-        pltpu.VMEM((ROWS, 128), F32),
+        pltpu.VMEM((2, ROWS, 128), BF16),
         pltpu.VMEM((n, ROWS, 128), BF16),
         pltpu.VMEM((depth, ROWS, 128), F32),
         pltpu.VMEM((2 * ROWS, 128), F32),
+        pltpu.SemaphoreType.DMA((2, 3)),
     ]
-    small_sems = [dma((k,)) for k in (1, 1, n - 1, n - 1, depth - 1, depth - 1, 1, 1)]
-    return large, large_sems, small, small_sems
+    return large, small
 
 
 def iota2(shape):
@@ -433,17 +371,16 @@
                 dot_nn(high[:, lanes], self.collect) + dot_nn(low[:, lanes], self.collect)
             ) * 0.125
 
-    def grad_two(self, acc, start):
-        at = pl.ds(pl.multiple_of(start, HALF), HALF)
+    def grad_two(self, acc, half):
         parts = []
         for fold in range(2):
             part = None
             for p in range(2):
-                first = pl.multiple_of(start + 288 * (p + 1) + 432 * fold, 16)
-                term = dot_nt(self.maps[pl.ds(first, HALF), :], self.g2s[64 * (p + 1) : 64 * (p + 2), :])
+                first = half * HALF + 288 * (p + 1) + 432 * fold
+                term = dot_nt(self.maps[first : first + HALF, :], self.g2s[64 * (p + 1) : 64 * (p + 2), :])
                 part = term if part is None else part + term
             parts.append(part)
-        acc[at, :] = jnp.concatenate(parts, axis=1)
+        acc[half * HALF : half * HALF + HALF, :] = jnp.concatenate(parts, axis=1)
 
     def back(self, plane):
         u = dot_nn(self.w3s[...], self.g2s[plane * 64 : plane * 64 + 192, :])
@@ -484,8 +421,8 @@
     halo = Halo(place, wide, cots, halo_send, halo_recv)
     halo.clear()
     local = Local(place.s, wide, cots, px, maps, z1s, g2s, g1s, w1s, w2s, w3s)
-    large = LargeFlow(place, *flows[0:6], flows[6:16])
-    small = SmallFlow(place, *flows[16:21], flows[21:29])
+    large = LargeFlow(place, *flows[0:6])
+    small = SmallFlow(place, *flows[6:12])
     fetched[0].wait()
     flatten_planes(crop_ref, wide, cf, lp, fs)
     fetched[1].wait()
@@ -520,9 +457,10 @@
     pair = local.second(1)
     pair = pair + local.second(2)
     local.features(pair, feats)
-    local.grad_two(large.acc, large.other)
-    large.halves()
-    local.grad_two(large.acc, large.mine)
+    local.grad_two(large.acc, 0)
+    large.shares(0)
+    local.grad_two(large.acc, 1)
+    large.shares(1)
     halo.wait(0, 1)
     local.patch(0, 1)
     local.first(0)
@@ -533,17 +471,14 @@
     local.first(5)
     halo.wait("right")
     local.second(3)
-    large.shares()
     local.back(0)
     local.back(1)
     local.grad_one(sel_ref, small.acc)
-    small.halves()
+    small.shares()
     feat_ref[...] = feats[...].T.astype(BF16)
-    small.plane()
     large.depth()
     large.gather()
     small.depth()
-    large.give_back()
     small.give_back()
     large.finish()
     two_ref[0:432, :] = large.fin[0:432, 0:64].astype(F32)
@@ -553,13 +488,22 @@
     for t in range(27):
         one_ref[t] = one[4 * t : 4 * t + 4]
     halo.drain()
-    for copy in large.sent + small.sent:
-        copy.wait_send()
+    large.drain()
+    small.drain()
+
+
+def store_kernel(*refs):
+    sems = refs[6]
+    copies = [pltpu.make_async_copy(refs[k], refs[3 + k], sems.at[k]) for k in range(3)]
+    for copy in copies:
+        copy.start()
+    for copy in copies:
+        copy.wait()
 
 
 def local(crop, filter_one, filter_two, cotangent):
     sel = jnp.asarray(tap_selection(), BF16)
-    large, large_sems, small, small_sems = flow_scratch()
+    large, small = flow_scratch()
     hbm = pl.BlockSpec(memory_space=pltpu.HBM)
     operands = (
         crop.reshape(1024, 64),
@@ -568,13 +512,14 @@
         sel,
         cotangent.transpose(0, 2, 3, 4, 1).reshape(256, 64),
     )
-    feat, one, two = pl.pallas_call(
+    shapes = (
+        jax.ShapeDtypeStruct((256, 64), BF16),
+        jax.ShapeDtypeStruct((27, 4, 32), F32),
+        jax.ShapeDtypeStruct((864, 64), F32),
+    )
+    results = pl.pallas_call(
         whole_kernel,
-        out_shape=(
-            jax.ShapeDtypeStruct((256, 64), BF16),
-            jax.ShapeDtypeStruct((27, 4, 32), F32),
-            jax.ShapeDtypeStruct((864, 64), F32),
-        ),
+        out_shape=shapes,
         in_specs=[hbm] * 5,
         scratch_shapes=[
             pltpu.VMEM((1024, 64), BF16),
@@ -601,14 +546,20 @@
             pltpu.SemaphoreType.DMA((10,)),
             pltpu.SemaphoreType.DMA((10,)),
             *large,
-            *large_sems,
             *small,
-            *small_sems,
         ],
         compiler_params=pltpu.CompilerParams(
             vmem_limit_bytes=32 * 1024 * 1024, collective_id=0, has_side_effects=True
         ),
     )(*[pltpu.with_memory_space_constraint(value, pltpu.HBM) for value in operands])
+    feat, one, two = pl.pallas_call(
+        store_kernel,
+        out_shape=shapes,
+        in_specs=[pl.BlockSpec(memory_space=pl.ANY)] * 3,
+        out_specs=[hbm] * 3,
+        scratch_shapes=[pltpu.SemaphoreType.DMA((3,))],
+        compiler_params=pltpu.CompilerParams(vmem_limit_bytes=1024 * 1024),
+    )(*results)
     feat = feat.reshape(1, 1, 16, 16, 64).transpose(0, 4, 1, 2, 3)
     return feat, one.reshape(3, 3, 3, 4, 32), two.reshape(3, 3, 3, 32, 64)
 

time: 39.9 us -> 34.9 us (0.87)
  Pallas kernels: 37.1 us -> 34.1 us
  local copies, waits for them, and re-layouts: 2.02 us -> 0 us
    pallas_call x1 -> x2, Pallas kernels: 37.1 us -> 34.1 us  [the longest x1 33.3 us: local(): pl.pallas_call(whole_kernel, out_shape=shapes, in_specs=[hbm] * 5, scratc...]
    unnamed x3 -> x0, local copies, waits for them, and re-layouts: 2.02 us -> none
where the time goes in v5:
time: 34.9 us; the launch traced here: 34.8 us
  Pallas kernels  34.1 us (98%)
  between operations  0.64 us (2%)
    pallas_call x1, Pallas kernels, local(): pl.pallas_call(whole_kernel, out_shape=shapes, in_specs=[hbm] * 5, scratc...  33.3 us
    pallas_call x1, Pallas kernels, local(): pl.pallas_call(store_kernel, out_shape=shapes, in_specs=[pl.BlockSpec(mem...  0.83 us

profile of v5, /device:TPU:1, one launch (start us, length us, event | category | flops | bytes accessed | tf_op | source)
XLA Modules:
  0.0 34.8 jit_solution(11163951447616244791)
XLA Ops:
  0.6 33.3 %shard_map.76 = (bf16[256,64]{1,0:T(8,128)(2,1)S(1)}, f32[27,4,32]{2,1,0:T(4,128)S(1)}, f32[864,64]{1,0:T(8,128)S(1)}) custom-call(bf16[1024,64]{1,0:T(8,128)(2,1)} %bitcast.11, bf16[27,4,32]{2,1,0:T(4,128)(2,1)} %bitcast.14, bf16[864,64]{1,0:T(8,128)(2,1)} %bitcast.12, bf16[128,2048]{1,0:T(8,128)(2,1)} %constant.2.clone.sel_hbm, bf16[256,64]{1,0:T(8,128)(2,1)} %bitcast.13), custom_call_target="tpu_custom_call" | custom-call | tf_op jit(solution)/shard_map/pallas_call | solution.py:520
  33.9 0.8 %shard_map.77 = (bf16[256,64]{1,0:T(8,128)(2,1)}, f32[27,4,32]{2,1,0:T(4,128)}, f32[864,64]{1,0:T(8,128)}) custom-call(bf16[256,64]{1,0:T(8,128)(2,1)S(1)} %get-tuple-element.9.refs_0_, f32[27,4,32]{2,1,0:T(4,128)S(1)} %get-tuple-element.10.refs_1_, f32[864,64]{1,0:T(8,128)S(1)} %get-tuple-element.11.refs_2_), custom_call_target="tpu_custom_call" | custom-call | tf_op jit(solution)/shard_map/pallas_call | solution.py:555

commit v6 on v5

--- a/solution.py
+++ b/solution.py
@@ -13,7 +13,7 @@
 
 
 def leaky(value):
-    return jnp.where(value > 0, value, 0.3 * value)
+    return jnp.maximum(value, 0.3 * value)
 
 
 def dot_nn(a, b):
@@ -106,6 +106,11 @@
     return sorted(range(1, count), key=lambda d: -min(d, count - d))
 
 
+def chip_offsets():
+    far = lambda d: min(d[0], NX - d[0]) + min(d[1], NY - d[1])
+    return sorted([(dx, dy) for dx in range(NX) for dy in range(NY)], key=lambda d: -far(d))
+
+
 def remote(src, dst, send, recv, peer):
     copy = pltpu.make_async_remote_copy(
         src_ref=src, dst_ref=dst, send_sem=send, recv_sem=recv, device_id=peer, device_id_type=MESH
@@ -197,14 +202,21 @@
     def shares(self, half):
         at = slice(half * HALF, half * HALF + HALF)
         self.accb[at, :] = self.acc[at, :].astype(BF16)
-        for k, (peer, core, row) in enumerate(self.peers):
-            go = remote(self.accb.at[rows16(row)], self.r1.at[k], self.sems.at[0, 0], self.sems.at[1, 0], peer)
-            pl.when(core == half)(go.start)
+        place = self.place
+        for k, (dx, dy) in enumerate(chip_offsets()):
+            x, y = (place.x + dx) % NX, (place.y + dy) % NY
+            src = self.accb.at[rows16(half * HALF + (x * NY + y) * ROWS)]
+            go = remote(src, self.r1.at[2 * k + place.core], self.sems.at[0, 0], self.sems.at[1, 0], place.at(x, y, place.z, half))
+            if (dx, dy) == (0, 0):
+                pl.when(place.core != half)(go.start)
+            else:
+                go.start()
 
     def depth(self):
-        self.arrive(0, self.r1)
-        total = self.acc[rows16(self.own), :]
-        for k in range(len(self.peers)):
+        self.arrive(0, self.r1.at[1:])
+        count = NX * NY - 1
+        total = self.acc[rows16(self.own), :] + self.r1[2 * count + 1 - self.place.core].astype(F32)
+        for k in range(2 * count):
             total = total + self.r1[k].astype(F32)
         self.r2[self.place.z] = total
         here = self.r2.at[self.place.z]
@@ -264,7 +276,7 @@
     large = [
         pltpu.VMEM((2 * HALF, 128), F32),
         pltpu.VMEM((2 * HALF, 128), BF16),
-        pltpu.VMEM((n - 1, ROWS, 128), BF16),
+        pltpu.VMEM((n, ROWS, 128), BF16),
         pltpu.VMEM((depth, ROWS, 128), F32),
         pltpu.VMEM((2 * HALF, 128), BF16),
         pltpu.SemaphoreType.DMA((2, 3)),
@@ -304,7 +316,8 @@
 
 
 class Local:
-    def __init__(self, s, wide, cots, px, maps, z1s, g2s, g1s, w1s, w2s, w3s):
+    def __init__(self, s, wide, cots, px, maps, z1s, g2s, g1s, w1s, w2s, w3s, widened):
+        self.widened = widened
         self.wide, self.cots, self.px, self.maps = wide, cots, px, maps
         self.z1s, self.g2s, self.g1s, self.w1s, self.w2s, self.w3s = z1s, g2s, g1s, w1s, w2s, w3s
         r, q = lane_masks(16)
@@ -358,10 +371,14 @@
 
     def second(self, plane):
         z = dot_nn(self.w2s[...], self.maps[plane * 288 : plane * 288 + 864, :])
-        cot = self.cots[(0, 1, 1, 2)[plane]]
-        wide = jnp.concatenate([dot_nn(cot[:, 0:128], self.spread), dot_nn(cot[:, 128:256], self.spread)], axis=1) * 0.125
+        wide = self.widened[...]
         self.g2s[plane * 64 : plane * 64 + 64, :] = jnp.where(z > 0, wide, 0.3 * wide).astype(BF16)
         return leaky(z)
+
+    def widen(self, which):
+        cot = self.cots[which]
+        self.widened[:, 0:512] = dot_nn(cot[:, 0:128], self.spread) * 0.125
+        self.widened[:, 512:1024] = dot_nn(cot[:, 128:256], self.spread) * 0.125
 
     def features(self, pair, feats):
         high, low = split2(pair)
@@ -371,16 +388,15 @@
                 dot_nn(high[:, lanes], self.collect) + dot_nn(low[:, lanes], self.collect)
             ) * 0.125
 
-    def grad_two(self, acc, half):
-        parts = []
-        for fold in range(2):
-            part = None
-            for p in range(2):
-                first = half * HALF + 288 * (p + 1) + 432 * fold
-                term = dot_nt(self.maps[first : first + HALF, :], self.g2s[64 * (p + 1) : 64 * (p + 2), :])
-                part = term if part is None else part + term
-            parts.append(part)
-        acc[half * HALF : half * HALF + HALF, :] = jnp.concatenate(parts, axis=1)
+    def grad_two(self, acc):
+        both = self.g2s[64:192, :]
+        low = dot_nt(self.maps[288:576, :], both[0:64])
+        mid = dot_nt(self.maps[576:1152, :], both)
+        high = dot_nt(self.maps[1152:1440, :], both[64:128])
+        acc[0:288, 0:64] = low + mid[0:288, 64:128]
+        acc[288:432, 0:64] = mid[0:144, 0:64] + mid[288:432, 64:128]
+        acc[0:144, 64:128] = mid[144:288, 0:64] + mid[432:576, 64:128]
+        acc[144:432, 64:128] = mid[288:576, 0:64] + high
 
     def back(self, plane):
         u = dot_nn(self.w3s[...], self.g2s[plane * 64 : plane * 64 + 192, :])
@@ -411,7 +427,7 @@
 
 def whole_kernel(crop_hbm, f1_hbm, f2_hbm, sel_hbm, cot_hbm, feat_ref, one_ref, two_ref,
                  crop_ref, f1_ref, f2_ref, sel_ref, cot_ref, wide, cots, px, maps, z1s, g2s, g1s,
-                 cf, lp, fs, f1s, w1s, w2s, w3s, feats, fetch, halo_send, halo_recv, *flows):
+                 cf, lp, fs, f1s, w1s, w2s, w3s, feats, widened, fetch, halo_send, halo_recv, *flows):
     place = Place()
     ready = greet(place)
     pairs = ((crop_hbm, crop_ref), (cot_hbm, cot_ref), (f1_hbm, f1_ref), (sel_hbm, sel_ref), (f2_hbm, f2_ref))
@@ -420,7 +436,7 @@
         copy.start()
     halo = Halo(place, wide, cots, halo_send, halo_recv)
     halo.clear()
-    local = Local(place.s, wide, cots, px, maps, z1s, g2s, g1s, w1s, w2s, w3s)
+    local = Local(place.s, wide, cots, px, maps, z1s, g2s, g1s, w1s, w2s, w3s, widened)
     large = LargeFlow(place, *flows[0:6])
     small = SmallFlow(place, *flows[6:12])
     fetched[0].wait()
@@ -441,35 +457,29 @@
     w2s[...] = f2_ref[...].astype(F32).T.astype(BF16)
     for a in range(3):
         w3s[:, 64 * a : 64 * a + 64] = f2_ref[288 * (2 - a) : 288 * (3 - a), :]
+    large.acc[432:512, :] = jnp.zeros((80, 128), F32)
     local.patch(5, 6, 7, 8)
-    halo.wait(4)
-    local.patch(4)
+    local.widen(1)
+    halo.wait(4, 9)
+    local.patch(4, 9)
     local.first(2)
-    halo.wait(9)
-    local.patch(9)
     local.first(3)
-    halo.wait(2)
-    local.patch(2, 3)
+    halo.wait(2, 10)
+    local.patch(2, 3, 10, 11)
     local.first(1)
-    halo.wait(10)
-    local.patch(10, 11)
     local.first(4)
-    pair = local.second(1)
-    pair = pair + local.second(2)
+    pair = local.second(1) + local.second(2)
+    local.grad_two(large.acc)
+    large.shares(0)
+    large.shares(1)
     local.features(pair, feats)
-    local.grad_two(large.acc, 0)
-    large.shares(0)
-    local.grad_two(large.acc, 1)
-    large.shares(1)
-    halo.wait(0, 1)
-    local.patch(0, 1)
+    halo.wait(0, 1, "left", 12, 13, "right")
+    local.patch(0, 1, 12, 13)
     local.first(0)
-    halo.wait("left")
+    local.first(5)
+    local.widen(0)
     local.second(0)
-    halo.wait(12, 13)
-    local.patch(12, 13)
-    local.first(5)
-    halo.wait("right")
+    local.widen(2)
     local.second(3)
     local.back(0)
     local.back(1)
@@ -542,6 +552,7 @@
             pltpu.VMEM((64, 864), BF16),
             pltpu.VMEM((288, 192), BF16),
             pltpu.VMEM((64, 256), F32),
+            pltpu.VMEM((64, LANES), F32),
             pltpu.SemaphoreType.DMA((5,)),
             pltpu.SemaphoreType.DMA((10,)),
             pltpu.SemaphoreType.DMA((10,)),

time: 34.9 us -> 33.9 us (0.971)
  Pallas kernels: 34.1 us -> 33.2 us
    pallas_call x1, Pallas kernels: 33.3 us -> 32.4 us  [local(): pl.pallas_call(whole_kernel, out_shape=shapes, in_specs=[hbm] * 5, scratc...]
where the time goes in v6:
time: 33.9 us; the launch traced here: 33.8 us
  Pallas kernels  33.2 us (98%)
  between operations  0.64 us (2%)
    pallas_call x1, Pallas kernels, local(): pl.pallas_call(whole_kernel, out_shape=shapes, in_specs=[hbm] * 5, scratc...  32.4 us
    pallas_call x1, Pallas kernels, local(): pl.pallas_call(store_kernel, out_shape=shapes, in_specs=[pl.BlockSpec(mem...  0.83 us

profile of v6, /device:TPU:1, one launch (start us, length us, event | category | flops | bytes accessed | tf_op | source)
XLA Modules:
  0.0 33.8 jit_solution(4469333943073433868)
XLA Ops:
  0.6 32.4 %shard_map.76 = (bf16[256,64]{1,0:T(8,128)(2,1)S(1)}, f32[27,4,32]{2,1,0:T(4,128)S(1)}, f32[864,64]{1,0:T(8,128)S(1)}) custom-call(bf16[1024,64]{1,0:T(8,128)(2,1)} %bitcast.11, bf16[27,4,32]{2,1,0:T(4,128)(2,1)} %bitcast.14, bf16[864,64]{1,0:T(8,128)(2,1)} %bitcast.12, bf16[128,2048]{1,0:T(8,128)(2,1)} %constant.2.clone.sel_hbm, bf16[256,64]{1,0:T(8,128)(2,1)} %bitcast.13), custom_call_target="tpu_custom_call" | custom-call | tf_op jit(solution)/shard_map/pallas_call | solution.py:530
  33.0 0.8 %shard_map.77 = (bf16[256,64]{1,0:T(8,128)(2,1)}, f32[27,4,32]{2,1,0:T(4,128)}, f32[864,64]{1,0:T(8,128)}) custom-call(bf16[256,64]{1,0:T(8,128)(2,1)S(1)} %get-tuple-element.9.refs_0_, f32[27,4,32]{2,1,0:T(4,128)S(1)} %get-tuple-element.10.refs_1_, f32[864,64]{1,0:T(8,128)S(1)} %get-tuple-element.11.refs_2_), custom_call_target="tpu_custom_call" | custom-call | tf_op jit(solution)/shard_map/pallas_call | solution.py:566

commit v7 on v6

--- a/solution.py
+++ b/solution.py
@@ -487,8 +487,8 @@
     small.shares()
     feat_ref[...] = feats[...].T.astype(BF16)
     large.depth()
+    small.depth()
     large.gather()
-    small.depth()
     small.give_back()
     large.finish()
     two_ref[0:432, :] = large.fin[0:432, 0:64].astype(F32)

time: 33.9 us -> 33 us (0.973)
  Pallas kernels: 33.2 us -> 32.2 us
    pallas_call x1, Pallas kernels: 32.4 us -> 31.4 us  [local(): pl.pallas_call(whole_kernel, out_shape=shapes, in_specs=[hbm] * 5, scratc...]
where the time goes in v7:
time: 33 us; the launch traced here: 32.9 us
  Pallas kernels  32.2 us (98%)
  between operations  0.64 us (2%)
    pallas_call x1, Pallas kernels, local(): pl.pallas_call(whole_kernel, out_shape=shapes, in_specs=[hbm] * 5, scratc...  31.4 us
    pallas_call x1, Pallas kernels, local(): pl.pallas_call(store_kernel, out_shape=shapes, in_specs=[pl.BlockSpec(mem...  0.83 us

profile of v7, /device:TPU:1, one launch (start us, length us, event | category | flops | bytes accessed | tf_op | source)
XLA Modules:
  0.0 32.9 jit_solution(16656650951506248532)
XLA Ops:
  0.6 31.4 %shard_map.76 = (bf16[256,64]{1,0:T(8,128)(2,1)S(1)}, f32[27,4,32]{2,1,0:T(4,128)S(1)}, f32[864,64]{1,0:T(8,128)S(1)}) custom-call(bf16[1024,64]{1,0:T(8,128)(2,1)} %bitcast.11, bf16[27,4,32]{2,1,0:T(4,128)(2,1)} %bitcast.14, bf16[864,64]{1,0:T(8,128)(2,1)} %bitcast.12, bf16[128,2048]{1,0:T(8,128)(2,1)} %constant.2.clone.sel_hbm, bf16[256,64]{1,0:T(8,128)(2,1)} %bitcast.13), custom_call_target="tpu_custom_call" | custom-call | tf_op jit(solution)/shard_map/pallas_call | solution.py:530
  32.0 0.8 %shard_map.77 = (bf16[256,64]{1,0:T(8,128)(2,1)}, f32[27,4,32]{2,1,0:T(4,128)}, f32[864,64]{1,0:T(8,128)}) custom-call(bf16[256,64]{1,0:T(8,128)(2,1)S(1)} %get-tuple-element.9.refs_0_, f32[27,4,32]{2,1,0:T(4,128)S(1)} %get-tuple-element.10.refs_1_, f32[864,64]{1,0:T(8,128)S(1)} %get-tuple-element.11.refs_2_), custom_call_target="tpu_custom_call" | custom-call | tf_op jit(solution)/shard_map/pallas_call | solution.py:566

commit v8 on v7

--- a/solution.py
+++ b/solution.py
@@ -65,34 +65,43 @@
 NX, NY, NZH, NZL = 4, 4, 2, 4
 ROWS = 16
 HALF = NX * NY * ROWS
-MESH = pl.DeviceIdType.MESH
+MESH = pl.DeviceIdType.LOGICAL
 
 
 class Place:
     def __init__(self):
-        dp, self.s = lax.axis_index("dp"), lax.axis_index("space")
-        self.zh, self.x = dp // NX, dp % NX
-        self.core = self.s % 2
-        self.y = self.s // 2 % NY
-        self.zl = self.s // 2 // NY
+        self.dp, self.s = lax.axis_index("dp"), lax.axis_index("space")
+        self.count = lax.axis_size("space")
+        self.zh, self.x = lax.div(self.dp, NX), lax.rem(self.dp, NX)
+        self.core = lax.rem(self.s, 2)
+        chip = lax.div(self.s, 2)
+        self.y, self.zl = lax.rem(chip, NY), lax.div(chip, NY)
         self.z = self.zh * NZL + self.zl
-
-    def at(self, x, y, z, core):
-        return {"dp": z // NZL * NX + x, "space": (z % NZL * NY + y) * 2 + core}
+        self.xs = [lax.rem(self.x + d, NX) for d in range(NX)]
+        self.ys = [lax.rem(self.y + d, NY) for d in range(NY)]
+        self.base = self.zh * (NX * self.count) + self.zl * (2 * NY)
+        self.columns = [self.base + x * self.count for x in self.xs]
+
+    def near(self, dx, dy, core):
+        return self.columns[dx] + self.ys[dy] * 2 + core
+
+    def along(self, hop):
+        return self.dp * self.count + lax.rem(self.s + hop + self.count, self.count)
 
     def plane_peers(self):
         peers = []
         for dx, dy, flip in plane_offsets():
-            x, y = (self.x + dx) % NX, (self.y + dy) % NY
             core = 1 - self.core if flip else self.core
-            peers.append((self.at(x, y, self.z, core), core, core * HALF + (x * NY + y) * ROWS))
+            peers.append((self.near(dx, dy, core), core, core * HALF + (self.xs[dx] * NY + self.ys[dy]) * ROWS))
         return peers
 
     def depth_peer(self, dz):
-        return self.at(self.x, self.y, (self.z + dz) % (NZH * NZL), self.core)
+        z = lax.rem(self.z + dz, NZH * NZL)
+        here = self.x * self.count + self.y * 2 + self.core
+        return here + lax.div(z, NZL) * (NX * self.count) + lax.rem(z, NZL) * (2 * NY)
 
     def partner(self):
-        return self.at(self.x, self.y, self.z, 1 - self.core)
+        return self.near(0, 0, 1 - self.core)
 
 
 def plane_offsets():
@@ -124,10 +133,9 @@
 
 def greet(place):
     barrier = pltpu.get_barrier_semaphore()
-    count = lax.axis_size("space")
     peers = [peer for peer, _, _ in place.plane_peers()]
     peers += [place.depth_peer(d) for d in depth_offsets()]
-    peers += [{"space": (place.s + hop + count) % count} for hop in (1, -1, 2, -2)]
+    peers += [place.along(hop) for hop in (1, -1, 2, -2)]
     for peer in peers:
         pl.semaphore_signal(barrier, inc=1, device_id=peer, device_id_type=MESH)
     return lambda: pl.semaphore_wait(barrier, len(peers))
@@ -138,7 +146,7 @@
 
 class Halo:
     def __init__(self, place, wide, cots, send, recv):
-        self.s, self.count = place.s, lax.axis_size("space")
+        self.place, self.s, self.count = place, place.s, place.count
         self.items = {}
         for k, (hop, own, planes, to) in enumerate(HALO_MOVES):
             self.add(to, hop, wide.at[5 + own : 5 + own + planes], wide.at[to : to + planes], send.at[k], recv.at[k])
@@ -147,7 +155,7 @@
                 self.add("right", -1, cots.at[1], cots.at[2], send.at[9], recv.at[9])
 
     def add(self, name, hop, src, dst, send, recv):
-        peer = {"space": (self.s + hop + self.count) % self.count}
+        peer = self.place.along(hop)
         self.items[name] = (hop, dst, remote(src, dst, send, recv, peer))
 
     def exists(self, hop):
@@ -173,6 +181,12 @@
     def drain(self):
         for hop, dst, copy in self.items.values():
             pl.when(self.exists(hop))(copy.wait_send)
+
+
+def tree_sum(terms):
+    while len(terms) > 1:
+        terms = [a + b for a, b in zip(terms[::2], terms[1::2])] + ([terms[-1]] if len(terms) % 2 else [])
+    return terms[0]
 
 
 class Flow:
@@ -204,9 +218,8 @@
         self.accb[at, :] = self.acc[at, :].astype(BF16)
         place = self.place
         for k, (dx, dy) in enumerate(chip_offsets()):
-            x, y = (place.x + dx) % NX, (place.y + dy) % NY
-            src = self.accb.at[rows16(half * HALF + (x * NY + y) * ROWS)]
-            go = remote(src, self.r1.at[2 * k + place.core], self.sems.at[0, 0], self.sems.at[1, 0], place.at(x, y, place.z, half))
+            src = self.accb.at[rows16(half * HALF + (place.xs[dx] * NY + place.ys[dy]) * ROWS)]
+            go = remote(src, self.r1.at[2 * k + place.core], self.sems.at[0, 0], self.sems.at[1, 0], place.near(dx, dy, half))
             if (dx, dy) == (0, 0):
                 pl.when(place.core != half)(go.start)
             else:
@@ -215,18 +228,16 @@
     def depth(self):
         self.arrive(0, self.r1.at[1:])
         count = NX * NY - 1
-        total = self.acc[rows16(self.own), :] + self.r1[2 * count + 1 - self.place.core].astype(F32)
-        for k in range(2 * count):
-            total = total + self.r1[k].astype(F32)
+        lanes = [self.acc[rows16(self.own), :], self.r1[2 * count + 1 - self.place.core].astype(F32)]
+        lanes += [self.r1[k].astype(F32) for k in range(2 * count)]
+        total = tree_sum(lanes)
         self.r2[self.place.z] = total
         here = self.r2.at[self.place.z]
         self.send(1, [(here, here, self.place.depth_peer(d)) for d in depth_offsets()])
 
     def gather(self):
         self.arrive(1, self.r2.at[1:])
-        total = self.r2[0]
-        for z in range(1, NZH * NZL):
-            total = total + self.r2[z]
+        total = tree_sum([self.r2[z] for z in range(NZH * NZL)])
         self.fin[rows16(self.own), :] = total.astype(BF16)
         here = self.fin.at[rows16(self.own)]
         self.send(2, [(here, here, peer) for peer, _, _ in self.peers])
@@ -251,18 +262,14 @@
 
     def depth(self):
         self.arrive(0, self.q1.at[1:])
-        total = self.q1[0].astype(F32)
-        for j in range(1, 2 * NX * NY):
-            total = total + self.q1[j].astype(F32)
+        total = tree_sum([self.q1[j].astype(F32) for j in range(2 * NX * NY)])
         self.q2[self.place.z] = total
         here = self.q2.at[self.place.z]
         self.send(1, [(here, here, self.place.depth_peer(d)) for d in depth_offsets()])
 
     def give_back(self):
         self.arrive(1, self.q2.at[1:])
-        total = self.q2[0]
-        for z in range(1, NZH * NZL):
-            total = total + self.q2[z]
+        total = tree_sum([self.q2[z] for z in range(NZH * NZL)])
         self.out[rows16(self.mine), :] = total
         here = self.out.at[rows16(self.mine)]
         self.send(2, [(here, here, self.place.partner())])
@@ -490,16 +497,16 @@
     small.depth()
     large.gather()
     small.give_back()
-    large.finish()
-    two_ref[0:432, :] = large.fin[0:432, 0:64].astype(F32)
-    two_ref[432:864, :] = large.fin[0:432, 64:128].astype(F32)
     small.finish()
     one = small.out[...].T
     for t in range(27):
         one_ref[t] = one[4 * t : 4 * t + 4]
     halo.drain()
+    small.drain()
+    large.finish()
+    two_ref[0:432, :] = large.fin[0:432, 0:64].astype(F32)
+    two_ref[432:864, :] = large.fin[0:432, 64:128].astype(F32)
     large.drain()
-    small.drain()
 
 
 def store_kernel(*refs):

time: 33 us -> 32.8 us (level)
  no operation moved by 1% of the time
where the time goes in v8:
time: 32.8 us; the launch traced here: 32.7 us
  Pallas kernels  32.1 us (98%)
  between operations  0.64 us (2%)
    pallas_call x1, Pallas kernels, local(): pl.pallas_call(whole_kernel, out_shape=shapes, in_specs=[hbm] * 5, scratc...  31.2 us
    pallas_call x1, Pallas kernels, local(): pl.pallas_call(store_kernel, out_shape=shapes, in_specs=[pl.BlockSpec(mem...  0.83 us

profile of v8, /device:TPU:1, one launch (start us, length us, event | category | flops | bytes accessed | tf_op | source)
XLA Modules:
  0.0 32.7 jit_solution(14285463960032375716)
XLA Ops:
  0.6 31.2 %shard_map.76 = (bf16[256,64]{1,0:T(8,128)(2,1)S(1)}, f32[27,4,32]{2,1,0:T(4,128)S(1)}, f32[864,64]{1,0:T(8,128)S(1)}) custom-call(bf16[1024,64]{1,0:T(8,128)(2,1)} %bitcast.11, bf16[27,4,32]{2,1,0:T(4,128)(2,1)} %bitcast.14, bf16[864,64]{1,0:T(8,128)(2,1)} %bitcast.12, bf16[128,2048]{1,0:T(8,128)(2,1)} %constant.2.clone.sel_hbm, bf16[256,64]{1,0:T(8,128)(2,1)} %bitcast.13), custom_call_target="tpu_custom_call" | custom-call | tf_op jit(solution)/shard_map/pallas_call | solution.py:537
  31.9 0.8 %shard_map.77 = (bf16[256,64]{1,0:T(8,128)(2,1)}, f32[27,4,32]{2,1,0:T(4,128)}, f32[864,64]{1,0:T(8,128)}) custom-call(bf16[256,64]{1,0:T(8,128)(2,1)S(1)} %get-tuple-element.9.refs_0_, f32[27,4,32]{2,1,0:T(4,128)S(1)} %get-tuple-element.10.refs_1_, f32[864,64]{1,0:T(8,128)S(1)} %get-tuple-element.11.refs_2_), custom_call_target="tpu_custom_call" | custom-call | tf_op jit(solution)/shard_map/pallas_call | solution.py:573

commit v9 on v8

--- a/solution.py
+++ b/solution.py
@@ -479,7 +479,6 @@
     local.grad_two(large.acc)
     large.shares(0)
     large.shares(1)
-    local.features(pair, feats)
     halo.wait(0, 1, "left", 12, 13, "right")
     local.patch(0, 1, 12, 13)
     local.first(0)
@@ -492,6 +491,7 @@
     local.back(1)
     local.grad_one(sel_ref, small.acc)
     small.shares()
+    local.features(pair, feats)
     feat_ref[...] = feats[...].T.astype(BF16)
     large.depth()
     small.depth()

time: 32.8 us -> 32.8 us (level)
  no operation moved by 1% of the time
where the time goes in v9:
time: 32.8 us; the launch traced here: 32.7 us
  Pallas kernels  32 us (98%)
  between operations  0.64 us (2%)
    pallas_call x1, Pallas kernels, local(): pl.pallas_call(whole_kernel, out_shape=shapes, in_specs=[hbm] * 5, scratc...  31.2 us
    pallas_call x1, Pallas kernels, local(): pl.pallas_call(store_kernel, out_shape=shapes, in_specs=[pl.BlockSpec(mem...  0.83 us

profile of v9, /device:TPU:1, one launch (start us, length us, event | category | flops | bytes accessed | tf_op | source)
XLA Modules:
  0.0 32.7 jit_solution(6515000638660147204)
XLA Ops:
  0.6 31.2 %shard_map.76 = (bf16[256,64]{1,0:T(8,128)(2,1)S(1)}, f32[27,4,32]{2,1,0:T(4,128)S(1)}, f32[864,64]{1,0:T(8,128)S(1)}) custom-call(bf16[1024,64]{1,0:T(8,128)(2,1)} %bitcast.11, bf16[27,4,32]{2,1,0:T(4,128)(2,1)} %bitcast.14, bf16[864,64]{1,0:T(8,128)(2,1)} %bitcast.12, bf16[128,2048]{1,0:T(8,128)(2,1)} %constant.2.clone.sel_hbm, bf16[256,64]{1,0:T(8,128)(2,1)} %bitcast.13), custom_call_target="tpu_custom_call" | custom-call | tf_op jit(solution)/shard_map/pallas_call | solution.py:537
  31.8 0.8 %shard_map.77 = (bf16[256,64]{1,0:T(8,128)(2,1)}, f32[27,4,32]{2,1,0:T(4,128)}, f32[864,64]{1,0:T(8,128)}) custom-call(bf16[256,64]{1,0:T(8,128)(2,1)S(1)} %get-tuple-element.9.refs_0_, f32[27,4,32]{2,1,0:T(4,128)S(1)} %get-tuple-element.10.refs_1_, f32[864,64]{1,0:T(8,128)S(1)} %get-tuple-element.11.refs_2_), custom_call_target="tpu_custom_call" | custom-call | tf_op jit(solution)/shard_map/pallas_call | solution.py:573
